TPU v7x, 32 devices: a whole 2x2x4 slice. The times are simulated.
32 devices in a mesh: space: 16 (over z, y, core), modes: 2 (over x).
Axes of the slice: x: 2, y: 2, z: 4, core: 2. Of those that a mesh axis runs over, the one named last changes fastest.
Arguments:
- initial_heat_weights: float32 [120, 16, 32, 128], P('modes', 'space'), may hold values from -6 to 6
- source_weights: float32 [120, 16, 32, 128], P('modes', 'space'), may hold values from -12 to 12
- heat_storage_slope: float32 [16, 32, 128], P('space'), may hold values from 1 to 8
- average_diffusivity: float32 [16, 32, 128], P('space'), may hold values from 0.5 to 2
- metal_indicator: int32 [16, 32, 128], P('space'), may hold values 0 or 1
- uncertain_diffusivity_fields: float32 [7, 16, 32, 128], P(None, 'space'), may hold values from -0.6 to 0.6
- basis_index_pairs: int32 [7, 72, 2], replicated, may hold values from 0 to 119
- basis_integral_entries: float32 [7, 72], replicated, may hold values from -3 to 3
Outputs:
- refined_heat_weights: float32 [120, 16, 32, 128], P('modes', 'space')
- residual: float32 [120, 16, 32, 128], P('modes', 'space')
Inputs may be any that keep to these rules, and one draw needn't show every extreme that they name: `basis_index_pairs`: pairs may repeat.
All inputs are finite; a program needn't handle non-finite values. No bound on the sum of `metal_indicator` on one device may be relied on, other than what follows from the above.
Results may differ from a plain program's by a relative error of at most 0.00024.
Values sent between devices are 32-bit elements; how exact they have to be, the bound alone decides.
No kernel may reach another device: no remote copies, remote signals or barrier semaphores. Data moves between devices by JAX's collectives and lax.ppermute only.
A program may use at most 64 MiB of HBM per device.

v0:
```python
import functools

import jax
import jax.numpy as jnp
from jax import lax
from jax.experimental import pallas as pl
from jax.experimental.pallas import tpu as pltpu
from jax.sharding import PartitionSpec as P


ROUNDS = 2
RELAXATION = 0.8
ROWS = 8
F32, BF16 = jnp.float32, jnp.bfloat16


def ceil_to(value, unit):
    return -(-value // unit) * unit


def group_of(n):
    return max(g for g in range(1, 7) if n % g == 0)


def params():
    return pltpu.CompilerParams(vmem_limit_bytes=6 * 1024 * 1024)


def vmem():
    return pl.BlockSpec(memory_space=pltpu.VMEM)


def cell_factors(chunk, slope, average, metal):
    at = pl.ds(chunk * ROWS, ROWS)
    here = slope[at, :]
    cond = average[at, :] * (1.0 + 3.0 * metal[at, :].astype(F32))
    return here, cond, RELAXATION * (1.0 / (here + 6.0 * cond))


def lap_kernel(n, chunk, slots, edge, compact, prev, cur, nxt, near, far, out):
    nz = cur.shape[1]
    g = group_of(n)
    row = lax.broadcasted_iota(jnp.int32, (g, ROWS, nz), 1)
    for j in range(0, n, g):

        def take(ref, slot):
            return ref[pl.ds((slot * n + j) * ROWS, g * ROWS), :].reshape(g, ROWS, nz)

        def handed(ref):
            rows = [ref[pl.ds(n * ROWS + j + i, 1), :] for i in range(g)]
            return jnp.stack([jnp.broadcast_to(r, (ROWS, nz)) for r in rows])

        x = take(cur, slots[1])
        if compact:
            before, after = handed(prev), handed(nxt)
        else:
            before = pltpu.roll(take(prev, slots[0]), 1, 1)
            after = pltpu.roll(take(nxt, slots[2]), ROWS - 1, 1)
        if len(near.shape) == 3:
            inside = near[pl.ds(j, g), pl.ds(chunk * ROWS, ROWS), :]
        else:
            inside = take(near, slots[3])
        up = jnp.where(row == 0, before, pltpu.roll(x, 1, 1))
        down = jnp.where(row == ROWS - 1, after, pltpu.roll(x, ROWS - 1, 1))
        sides = pltpu.roll(x, 1, 2) + pltpu.roll(x, nz - 1, 2)
        beside = (up + down) + sides + (inside + take(far, slots[4]))
        out[pl.ds(j * ROWS, g * ROWS), :] = (6.0 * x - beside).reshape(g * ROWS, nz)
    if edge is not None:
        start = slots[1] * n * ROWS + edge
        out[pl.ds(n * ROWS, n), :] = cur[pl.ds(start, n, stride=ROWS), :]


def couple(n, chunk, blocks, fields, matrix, lap, rhs, mixed, emit):
    nz = lap.shape[1]
    kl = fields.shape[0]
    wide, tall = ceil_to(n, 16), ceil_to(n, 8)
    used = pl.ds(0, blocks * kl * tall)
    for pair in range(ROWS // 2):
        slot = pair % 2
        for half in range(2):
            v = lap[pl.ds(2 * pair + half, n, stride=ROWS), :]
            hi = v.astype(BF16)
            lo = (v - hi.astype(F32)).astype(BF16)
            cols = pl.ds(half * nz, nz)
            rhs[slot, pl.ds(0, n), cols] = hi
            rhs[slot, pl.ds(wide, n), cols] = lo
            rhs[slot, pl.ds(2 * wide, n), cols] = hi
        mixed[slot] = jnp.dot(matrix[used, :], rhs[slot], preferred_element_type=F32)
        for half in range(2):
            y = 2 * pair + half
            cols = pl.ds(half * nz, nz)
            for b in range(blocks):
                total = None
                for k in range(kl):
                    field = fields[k, pl.ds(chunk * ROWS + y, 1), :]
                    at = pl.ds((b * kl + k) * tall, n)
                    term = field * mixed[slot, at, cols]
                    total = term if total is None else total + term
                emit(y, b, total)


def clear_rhs(n, rhs):
    if ceil_to(n, 16) != n:
        rhs[...] = jnp.zeros_like(rhs)


def own_kernel(n, chunk, blocks, fields, matrices, lap, out, rhs, mixed):
    clear_rhs(n, rhs)

    def emit(y, b, total):
        out[pl.ds(b * n * ROWS + y, n, stride=ROWS), :] = total

    couple(n, chunk, blocks, fields, matrices.at[0], lap, rhs, mixed, emit)


def blend_kernel(n, chunk, slope, average, metal, field, source, out):
    nz = field.shape[1]
    here, _, step = cell_factors(chunk, slope, average, metal)
    g = group_of(n)
    for j in range(0, n, g):
        rows = pl.ds(j * ROWS, g * ROWS)
        u = field[rows, :].reshape(g, ROWS, nz)
        v = u + step * (source[pl.ds(j, g)] - here * u)
        out[rows, :] = v.reshape(g * ROWS, nz)


def final_kernel(n, chunk, slot, others, last, double, *refs):
    fields, slope, average, metal, matrices, source, field, lap, own = refs[:9]
    laps, refs = refs[9 : 9 + others], refs[9 + others :]
    blended, refs = (refs[0], refs[1:]) if double else (None, refs)
    outs, (rhs, mixed, sums) = refs[:-3], refs[-3:]
    outs = outs[2:] if len(outs) == 4 else outs
    nz = lap.shape[1]
    clear_rhs(n, rhs)
    for other in range(others):
        base = own if other == 0 else sums

        def emit(y, b, total):
            at = pl.ds(b * n * ROWS + y, n, stride=ROWS)
            sums[at, :] = base[at, :] + total

        blocks = 2 if double else 1
        couple(
            n, chunk, blocks, fields, matrices.at[1 + other], laps[other], rhs, mixed, emit
        )
    here, cond, step = cell_factors(chunk, slope, average, metal)
    g = group_of(n)
    for j in range(0, n, g):

        def take(ref, part=0):
            rows = pl.ds((part * n + j) * ROWS, g * ROWS)
            return ref[rows, :].reshape(g, ROWS, nz)

        u = take(field, slot)
        residual = source[pl.ds(j, g)] - (here * u + (cond * take(lap) + take(sums)))
        u = u + step * residual
        if last:
            outs[0][pl.ds(j, g)] = u
            outs[1][pl.ds(j, g)] = residual
        else:
            outs[0][pl.ds(j * ROWS, g * ROWS), :] = u.reshape(g * ROWS, nz)
        if double:
            u = take(blended) - step * (cond * take(laps[0]) + take(sums, 1))
            outs[0][pl.ds((n + j) * ROWS, g * ROWS), :] = u.reshape(g * ROWS, nz)


def matrices_kernel(n, count, blocks, me, pairs, entries, out):
    kl, _, listed = pairs.shape
    wide, tall = ceil_to(n, 16), ceil_to(n, 8)
    row = lax.broadcasted_iota(jnp.int32, (tall, listed), 0)
    column = lax.broadcasted_iota(jnp.int32, (wide, listed), 0)
    starts = [lax.rem(me[0] - s + count, count) * n for s in range(count)]
    columns = jnp.concatenate(
        [jnp.where(column < n, start + column, -1) for start in starts], axis=0
    )
    for k in range(kl):
        hits = jnp.where(columns == pairs[k, pl.ds(1, 1), :], 1.0, 0.0).astype(BF16)
        for b in range(blocks):
            rows = jnp.where(row < n, starts[b] + row, -1)
            value = jnp.broadcast_to(entries[pl.ds(k, 1), :], (tall, listed))
            value = jnp.where(rows == pairs[k, pl.ds(0, 1), :], value, 0.0)
            parts = []
            for _ in range(3):
                part = value.astype(BF16)
                value = value - part.astype(F32)
                parts.append(part)
            sums = lax.dot_general(
                jnp.concatenate(parts, axis=0),
                hits,
                (((1,), (1,)), ((), ())),
                preferred_element_type=F32,
            )
            g = sums[:tall] + sums[tall : 2 * tall] + sums[2 * tall :]
            hi = g.astype(BF16)
            lo = (g - hi.astype(F32)).astype(BF16)
            for s in range(count):
                at = slice(s * wide, (s + 1) * wide)
                out[s, pl.ds((b * kl + k) * tall, tall), :] = jnp.concatenate(
                    [hi[:, at], hi[:, at], lo[:, at]], axis=1
                )


def whole(a):
    return pl.BlockSpec(a.shape, lambda i, d=len(a.shape): (0,) * d)


def rows_of(a, chunk):
    return pl.BlockSpec((a.shape[0], ROWS, a.shape[2]), lambda i: (0, chunk, 0))


def estimate(flops, moved):
    return pl.CostEstimate(flops=flops, bytes_accessed=4 * moved, transcendentals=0)


def scratch(n, blocks, kl, nz):
    wide, tall = ceil_to(n, 16), ceil_to(n, 8)
    return [
        pltpu.VMEM((2, 3 * wide, 2 * nz), BF16),
        pltpu.VMEM((2, blocks * kl * tall, 2 * nz), F32),
    ]


def lap_call(n, chunk, prev, cur, nxt, near, far, edge=None, compact=False):
    arrays, slots = zip(prev, cur, nxt, near, far)
    nz = cur[0].shape[1]
    rows = n * ROWS + (0 if edge is None else n)
    return pl.pallas_call(
        functools.partial(lap_kernel, n, chunk, slots, edge, compact),
        out_shape=jax.ShapeDtypeStruct((rows, nz), F32),
        in_specs=[vmem()] * 5,
        out_specs=vmem(),
        compiler_params=params(),
        name="lap",
        cost_estimate=estimate(12 * rows * nz, 6 * rows * nz),
    )(*arrays)


def own_call(n, chunk, blocks, fields, matrices, lap):
    kl, _, nz = fields.shape
    size = n * ROWS * nz
    return pl.pallas_call(
        functools.partial(own_kernel, n, chunk, blocks),
        out_shape=jax.ShapeDtypeStruct((blocks * n * ROWS, nz), F32),
        in_specs=[vmem()] * 3,
        out_specs=vmem(),
        scratch_shapes=scratch(n, blocks, kl, nz),
        compiler_params=params(),
        name="own",
        cost_estimate=estimate(6 * blocks * kl * n * size, 2 * size),
    )(fields, matrices, lap)


def blend_call(n, chunk, shared, field, source):
    nz = field.shape[1]
    size = n * ROWS * nz
    operands = [*shared[1:], field, source]
    return pl.pallas_call(
        functools.partial(blend_kernel, n, chunk),
        grid=(1,),
        out_shape=jax.ShapeDtypeStruct((n * ROWS, nz), F32),
        in_specs=[*(whole(a) for a in operands[:-1]), rows_of(source, chunk)],
        out_specs=pl.BlockSpec((n * ROWS, nz), lambda i: (0, 0)),
        compiler_params=params(),
        name="blend",
        cost_estimate=estimate(4 * size, 3 * size),
    )(*operands)


def final_call(n, chunk, last, shared, matrices, source, field, lap, own, laps, blended, outs):
    nz = source.shape[2]
    double = blended is not None
    blocks = 2 if double else 1
    operands = [*shared, matrices, source, field[0], lap, own, *laps]
    operands += [blended] if double else []
    specs = [rows_of(a, chunk) if a is source else whole(a) for a in operands]
    aliases = {}
    if last:
        shapes = [jax.ShapeDtypeStruct(source.shape, F32)] * 2
        out_specs = [rows_of(source, chunk)] * 2
        if outs:
            aliases = {len(operands) + i: i for i in range(2)}
            operands += list(outs)
            specs += [pl.BlockSpec(memory_space=pl.ANY)] * 2
    else:
        shapes = [jax.ShapeDtypeStruct((blocks * n * ROWS, nz), F32)]
        out_specs = [whole(shapes[0])]
    size = n * ROWS * nz
    kl = shared[0].shape[0]
    return pl.pallas_call(
        functools.partial(final_kernel, n, chunk, field[1], len(laps), last, double),
        grid=(1,),
        out_shape=shapes,
        in_specs=specs,
        out_specs=out_specs,
        scratch_shapes=[
            *scratch(n, blocks, kl, nz),
            pltpu.VMEM((blocks * n * ROWS, nz), F32),
        ],
        input_output_aliases=aliases,
        compiler_params=params(),
        name="final",
        cost_estimate=estimate(6 * blocks * len(laps) * kl * n * size, 6 * size),
    )(*operands)


def coupling(pairs, entries, n, blocks):
    count = lax.axis_size("modes")
    me = lax.axis_index("modes").astype(jnp.int32).reshape(1)
    kl, listed = entries.shape
    wide, tall = ceil_to(n, 16), ceil_to(n, 8)
    shape = (count, blocks * kl * tall, 3 * wide)
    return pl.pallas_call(
        functools.partial(matrices_kernel, n, count, blocks),
        out_shape=jax.ShapeDtypeStruct(shape, BF16),
        in_specs=[pl.BlockSpec(memory_space=pltpu.SMEM), vmem(), vmem()],
        out_specs=vmem(),
        compiler_params=params(),
        name="coupling",
        cost_estimate=estimate(2 * listed * shape[0] * shape[1] * shape[2], 10000),
    )(me, pairs.transpose(0, 2, 1), entries)


def near_swap(x):
    count = lax.axis_size("space")
    return lax.ppermute(x, "space", [(i, i ^ 1) for i in range(count)])


def far_swap(x):
    count = lax.axis_size("space")
    pairs = [(i, (i + (1 if i % 2 else -1)) % count) for i in range(count)]
    return lax.ppermute(x, "space", pairs)


def to_others(x):
    count = lax.axis_size("modes")
    got = []
    for s in range(1, count):
        ring = [(i, (i + s) % count) for i in range(count)]
        got.append(lax.ppermute(x, "modes", ring))
    return got


FINALS = (1, 0, 2, 3)


def doubled(count, devices):
    return count == 4 and devices == 2


def rounds(n, count, u0, source, shared, pairs, entries):
    nz = u0.shape[-1]
    double = doubled(count, lax.axis_size("modes"))
    tail = count - 1
    cut = lambda c: u0[:, c * ROWS : (c + 1) * ROWS].reshape(n * ROWS, nz)
    field = {0: (cut(0), 0)}
    u0, first = lax.optimization_barrier((u0, field[0][0]))
    field[0] = (first, 0)
    for c in range(1, count):
        field[c] = (cut(c), 0)
    matrices = coupling(pairs, entries, n, 2 if double else 1)
    near_whole = near_swap(u0)
    blended = None
    if double:
        blended = blend_call(n, tail, shared, field[tail][0], source)
        (blended,) = to_others(blended)
    outs = ()
    for turn in range(ROUNDS):
        last = turn == ROUNDS - 1
        near, far, parts = {}, {}, {}
        for c in range(count):
            if turn:
                near[c] = (near_swap(field[c][0]), 0)
            else:
                near[c] = (near_whole, 0)
            far[c] = (far_swap(field[c][0]), 0)
        for c in range(count):
            both = double and c == tail
            prev, nxt = field[(c - 1) % count], field[(c + 1) % count]
            edge = None
            if double and last and not both:
                edge = {(tail - 1): ROWS - 1, (tail + 1) % count: 0}.get(c)
            lap = lap_call(n, c, prev, field[c], nxt, near[c], far[c], edge)
            if both and last:
                of_other = lambda a: (a[0], 1)
                handed = [(parts[d % count][3][0], 0) for d in (tail - 1, tail + 1)]
                laps = [
                    lap_call(
                        n,
                        c,
                        handed[0],
                        of_other(field[c]),
                        handed[1],
                        of_other(near[c]),
                        of_other(far[c]),
                        compact=True,
                    )
                ]
            else:
                laps = to_others(lap)
            blocks = 2 if both and not last else 1
            own = own_call(n, c, blocks, shared[0], matrices, lap)
            parts[c] = (field[c], lap, own, laps)
        new = {}
        for c in FINALS if last and double else range(count):
            given = blended if double and c == tail and not last else None
            got = final_call(
                n, c, last, shared, matrices, source, *parts[c], given, outs
            )
            if last:
                outs = got
            else:
                new[c] = (got[0], 0)
        field = new
    return outs


def on_device(
    initial_heat_weights,
    source_weights,
    heat_storage_slope,
    average_diffusivity,
    metal_indicator,
    uncertain_diffusivity_fields,
    basis_index_pairs,
    basis_integral_entries,
):
    n, planes, ny, _ = initial_heat_weights.shape
    assert planes == 1 and ny % ROWS == 0
    u0 = initial_heat_weights[:, 0]
    source = source_weights[:, 0]
    shared = (
        uncertain_diffusivity_fields[:, 0],
        heat_storage_slope[0],
        average_diffusivity[0],
        metal_indicator[0],
    )
    outs = rounds(
        n, ny // ROWS, u0, source, shared, basis_index_pairs, basis_integral_entries
    )
    return (outs[0][:, None], outs[1][:, None])


def solution(mesh):
    placed = (
        P("modes", "space", None, None),
        P("modes", "space", None, None),
        P("space", None, None),
        P("space", None, None),
        P("space", None, None),
        P(None, "space", None, None),
        P(),
        P(),
    )
    return jax.shard_map(
        on_device,
        mesh=mesh,
        in_specs=placed,
        out_specs=(P("modes", "space", None, None), P("modes", "space", None, None)),
        check_vma=False,
    )
```

profile of v0, /device:TPU:1, one launch (start us, length us, event | category | flops | bytes accessed | tf_op | source)
XLA Modules:
  0.0 79.6 jit_solution(12584627038103702308)
XLA Ops:
  1.7 2.7 %collective-permute-start.6 = (f32[480,128]{1,0:T(8,128)S(1)}, f32[480,128]{1,0:T(8,128)S(1)}, u32[]{:S(2)}, u32[]{:S(2)}) collective-permute-start(f32[480,128]{1,0:T(8,128)S(1)} %slice_bitcast_fusion.nxt.cur.refs_6_.prev), channel_id=1, source_target_pairs={{0,30},{2,4},{4,2},{6,8},{8,6},{10,12},{12,10},{14,16},{16,14},{18... | collective-permute-start | bytes 737288 | tf_op jit(solution)/shard_map/ppermute | solution.py:331
  4.4 1.2 %slice_bitcast_fusion.1 = (f32[480,128]{1,0:T(8,128)S(1)}, f32[480,128]{1,0:T(8,128)S(1)}, f32[480,128]{1,0:T(8,128)S(1)}) fusion(f32[60,32,128]{2,1,0:T(8,128)} %bitcast.79), kind=kLoop, calls=%fused_computation.1 | loop fusion | bytes 1474560 | tf_op jit(solution)/shard_map/reshape | solution.py:354
  5.7 1.7 %collective-permute-start.10 = (f32[480,128]{1,0:T(8,128)S(1)}, f32[480,128]{1,0:T(8,128)S(1)}, u32[]{:S(2)}, u32[]{:S(2)}) collective-permute-start(f32[480,128]{1,0:T(8,128)S(1)} %get-tuple-element.24.prev.nxt.cur.refs_6_), channel_id=1, source_target_pairs={{0,30},{2,4},{4,2},{6,8},{8,6},{10,12},{12,10},{14,16},{16,14},{18... | collective-permute-start | bytes 737288 | tf_op jit(solution)/shard_map/ppermute | solution.py:331
  7.5 10.5 %collective-permute-done.6.far = f32[480,128]{1,0:T(8,128)S(1)} collective-permute-done((f32[480,128]{1,0:T(8,128)S(1)}, f32[480,128]{1,0:T(8,128)S(1)}, u32[]{:S(2)}, u32[]{:S(2)}) %collective-permute-start.6) | collective-permute-done | bytes 245792 | tf_op jit(solution)/shard_map/ppermute | solution.py:331
  18.9 1.2 %collective-permute-start.7 = (f32[480,128]{1,0:T(8,128)}, f32[480,128]{1,0:T(8,128)}, u32[]{:S(2)}, u32[]{:S(2)}) collective-permute-start(f32[480,128]{1,0:T(8,128)} %lap.11.refs_7_), channel_id=1, source_target_pairs={{0,1},{1,0},{2,3},{3,2},{4,5},{5,4},{6,7},{7,6},{8,9},{9,8},{10,11... | collective-permute-start | bytes 737288 | tf_op jit(solution)/shard_map/ppermute | solution.py:339
  20.9 1.3 %collective-permute-start.5 = (f32[480,128]{1,0:T(8,128)S(1)}, f32[480,128]{1,0:T(8,128)}, u32[]{:S(2)}, u32[]{:S(2)}) collective-permute-start(f32[480,128]{1,0:T(8,128)S(1)} %lap.10.refs_7_), channel_id=1, source_target_pairs={{0,1},{1,0},{2,3},{3,2},{4,5},{5,4},{6,7},{7,6},{8,9},{9,8},{10,11... | collective-permute-start | bytes 737288 | tf_op jit(solution)/shard_map/ppermute | solution.py:339
  22.2 2.4 %collective-permute-done.10.far = f32[480,128]{1,0:T(8,128)S(1)} collective-permute-done((f32[480,128]{1,0:T(8,128)S(1)}, f32[480,128]{1,0:T(8,128)S(1)}, u32[]{:S(2)}, u32[]{:S(2)}) %collective-permute-start.10) | collective-permute-done | bytes 245792 | tf_op jit(solution)/shard_map/ppermute | solution.py:331
  24.8 1.7 %collective-permute-start.11 = (f32[480,128]{1,0:T(8,128)S(1)}, f32[480,128]{1,0:T(8,128)}, u32[]{:S(2)}, u32[]{:S(2)}) collective-permute-start(f32[480,128]{1,0:T(8,128)S(1)} %lap.13.refs_7_), channel_id=1, source_target_pairs={{0,1},{1,0},{2,3},{3,2},{4,5},{5,4},{6,7},{7,6},{8,9},{9,8},{10,11... | collective-permute-start | bytes 737288 | tf_op jit(solution)/shard_map/ppermute | solution.py:339
  30.5 1.4 %own.10.refs_8_ = f32[480,128]{1,0:T(8,128)S(1)} custom-call(f32[7,32,128]{2,1,0:T(8,128)S(1)} %bitcast.31, bf16[2,896,192]{2,1,0:T(8,128)(2,1)S(1)} %coupling.1.matrices.refs_4_, f32[480,128]{1,0:T(8,128)} %lap.11.refs_7_), custom_call_target="tpu_custom_call" | custom-call | flops 154828800 | bytes 491520 | tf_op jit(solution)/shard_map/own/pallas_call | solution.py:241
  32.5 1.7 %final.10.nxt.cur.prev.refs_6_ = f32[480,128]{1,0:T(8,128)S(1)} custom-call(f32[7,32,128]{2,1,0:T(8,128)S(1)} %bitcast.33, f32[32,128]{1,0:T(8,128)S(1)} %bitcast.48, f32[32,128]{1,0:T(8,128)S(1)} %bitcast.57, s32[32,128]{1,0:T(8,128)S(1)} %bitcast.66, bf16[2,896,192]{2,1,0:T(8,128)(2,1)S(1)} %coupling.1.matrices.refs_4_, f32[60,32,128]{2,1,0:T(8,128)S(1)} %bitcast.23, ...), custom_call_target="tpu_custom_call" | custom-call | flops 154828800 | bytes 1474560 | tf_op jit(solution)/shard_map/final/pallas_call | solution.py:289
  34.3 1.7 %collective-permute-start.16 = (f32[480,128]{1,0:T(8,128)S(1)}, f32[480,128]{1,0:T(8,128)S(1)}, u32[]{:S(2)}, u32[]{:S(2)}) collective-permute-start(f32[480,128]{1,0:T(8,128)S(1)} %final.10.nxt.cur.prev.refs_6_), channel_id=1, source_target_pairs={{0,30},{2,4},{4,2},{6,8},{8,6},{10,12},{12,10},{14,16},{16,14},{18... | collective-permute-start | bytes 737288 | tf_op jit(solution)/shard_map/ppermute | solution.py:331
  36.0 1.6 %final.9.prev.cur.nxt.refs_6_ = f32[480,128]{1,0:T(8,128)S(1)} custom-call(f32[7,32,128]{2,1,0:T(8,128)S(1)} %bitcast.34, f32[32,128]{1,0:T(8,128)S(1)} %bitcast.49, f32[32,128]{1,0:T(8,128)S(1)} %bitcast.58, s32[32,128]{1,0:T(8,128)S(1)} %bitcast.67, bf16[2,896,192]{2,1,0:T(8,128)(2,1)S(1)} %coupling.1.matrices.refs_4_, f32[60,32,128]{2,1,0:T(8,128)S(1)} %bitcast.24, ...), custom_call_target="tpu_custom_call" | custom-call | flops 154828800 | bytes 1474560 | tf_op jit(solution)/shard_map/final/pallas_call | solution.py:289
  37.7 3.5 %collective-permute-start.12 = (f32[480,128]{1,0:T(8,128)S(1)}, f32[480,128]{1,0:T(8,128)S(1)}, u32[]{:S(2)}, u32[]{:S(2)}) collective-permute-start(f32[480,128]{1,0:T(8,128)S(1)} %final.9.prev.cur.nxt.refs_6_), channel_id=1, source_target_pairs={{0,2},{2,0},{4,6},{6,4},{8,10},{10,8},{12,14},{14,12},{16,18},{18,... | collective-permute-start | bytes 737288 | tf_op jit(solution)/shard_map/ppermute | solution.py:325
  42.4 1.6 %final.11.prev.nxt.cur.refs_6_ = f32[480,128]{1,0:T(8,128)S(1)} custom-call(f32[7,32,128]{2,1,0:T(8,128)S(1)} %bitcast.37, f32[32,128]{1,0:T(8,128)S(1)} %bitcast.50, f32[32,128]{1,0:T(8,128)S(1)} %bitcast.59, s32[32,128]{1,0:T(8,128)S(1)} %bitcast.68, bf16[2,896,192]{2,1,0:T(8,128)(2,1)S(1)} %coupling.1.matrices.refs_4_, f32[60,32,128]{2,1,0:T(8,128)S(1)} %bitcast.25, ...), custom_call_target="tpu_custom_call" | custom-call | flops 154828800 | bytes 1474560 | tf_op jit(solution)/shard_map/final/pallas_call | solution.py:289
  44.4 1.8 %collective-permute-start.18 = (f32[480,128]{1,0:T(8,128)S(1)}, f32[480,128]{1,0:T(8,128)S(1)}, u32[]{:S(2)}, u32[]{:S(2)}) collective-permute-start(f32[480,128]{1,0:T(8,128)S(1)} %final.11.prev.nxt.cur.refs_6_), channel_id=1, source_target_pairs={{0,2},{2,0},{4,6},{6,4},{8,10},{10,8},{12,14},{14,12},{16,18},{18,... | collective-permute-start | bytes 737288 | tf_op jit(solution)/shard_map/ppermute | solution.py:325
  46.2 1.9 %final.8.cur.nxt.prev.refs_6_ = f32[960,128]{1,0:T(8,128)S(1)} custom-call(f32[7,32,128]{2,1,0:T(8,128)S(1)} %bitcast.38, f32[32,128]{1,0:T(8,128)S(1)} %bitcast.51, f32[32,128]{1,0:T(8,128)S(1)} %bitcast.60, s32[32,128]{1,0:T(8,128)S(1)} %bitcast.69, bf16[2,896,192]{2,1,0:T(8,128)(2,1)S(1)} %coupling.1.matrices.refs_4_, f32[60,32,128]{2,1,0:T(8,128)S(1)} %bitcast.26, ...), custom_call_target="tpu_custom_call" | custom-call | flops 309657600 | bytes 1474560 | tf_op jit(solution)/shard_map/final/pallas_call | solution.py:289
  48.4 1.7 %collective-permute-start.19 = (f32[480,128]{1,0:T(8,128)S(1)}, f32[480,128]{1,0:T(8,128)S(1)}, u32[]{:S(2)}, u32[]{:S(2)}) collective-permute-start(f32[480,128]{1,0:T(8,128)S(1)} %final.11.prev.nxt.cur.refs_6_), channel_id=1, source_target_pairs={{0,30},{2,4},{4,2},{6,8},{8,6},{10,12},{12,10},{14,16},{16,14},{18... | collective-permute-start | bytes 737288 | tf_op jit(solution)/shard_map/ppermute | solution.py:331
  50.3 2.1 %collective-permute-done.13.far = f32[480,128]{1,0:T(8,128)S(1)} collective-permute-done((f32[480,128]{1,0:T(8,128)S(1)}, f32[480,128]{1,0:T(8,128)S(1)}, u32[]{:S(2)}, u32[]{:S(2)}) %collective-permute-start.13) | collective-permute-done | bytes 245792 | tf_op jit(solution)/shard_map/ppermute | solution.py:331
  54.1 14.3 %collective-permute-done.19.far = f32[480,128]{1,0:T(8,128)S(1)} collective-permute-done((f32[480,128]{1,0:T(8,128)S(1)}, f32[480,128]{1,0:T(8,128)S(1)}, u32[]{:S(2)}, u32[]{:S(2)}) %collective-permute-start.19) | collective-permute-done | bytes 245792 | tf_op jit(solution)/shard_map/ppermute | solution.py:331
  71.4 2.4 %collective-permute-done.20.refs_9_ = f32[480,128]{1,0:T(8,128)S(1)} collective-permute-done((f32[480,128]{1,0:T(8,128)S(1)}, f32[480,128]{1,0:T(8,128)S(1)}, u32[]{:S(2)}, u32[]{:S(2)}) %collective-permute-start.20) | collective-permute-done | bytes 245792 | tf_op jit(solution)/shard_map/ppermute | solution.py:339
  73.8 1.4 %final.12 = (f32[60,32,128]{2,1,0:T(8,128)}, f32[60,32,128]{2,1,0:T(8,128)}) custom-call(f32[7,32,128]{2,1,0:T(8,128)S(1)} %bitcast.43, f32[32,128]{1,0:T(8,128)S(1)} %bitcast.52, f32[32,128]{1,0:T(8,128)S(1)} %bitcast.61, s32[32,128]{1,0:T(8,128)S(1)} %bitcast.70, bf16[2,896,192]{2,1,0:T(8,128)(2,1)S(1)} %coupling.1.matrices.refs_4_, ...), custom_call_target="tpu_custom_call" | custom-call | flops 154828800 | bytes 1474560 | tf_op jit(solution)/shard_map/final/pallas_call | solution.py:289
  75.4 1.4 %final.13 = (f32[60,32,128]{2,1,0:T(8,128)}, f32[60,32,128]{2,1,0:T(8,128)}) custom-call(f32[7,32,128]{2,1,0:T(8,128)S(1)} %bitcast.44, f32[32,128]{1,0:T(8,128)S(1)} %bitcast.53, f32[32,128]{1,0:T(8,128)S(1)} %bitcast.62, s32[32,128]{1,0:T(8,128)S(1)} %bitcast.71, ...), custom_call_target="tpu_custom_call", output_to_operand_aliasing={{0}: (10, {}), {1}: (11, {})} | custom-call | flops 154828800 | bytes 1474560 | tf_op jit(solution)/shard_map/final/pallas_call | solution.py:289
  76.8 1.4 %final.14 = (f32[60,32,128]{2,1,0:T(8,128)}, f32[60,32,128]{2,1,0:T(8,128)}) custom-call(f32[7,32,128]{2,1,0:T(8,128)S(1)} %bitcast.45, f32[32,128]{1,0:T(8,128)S(1)} %bitcast.54, f32[32,128]{1,0:T(8,128)S(1)} %bitcast.63, s32[32,128]{1,0:T(8,128)S(1)} %bitcast.72, ...), custom_call_target="tpu_custom_call", output_to_operand_aliasing={{0}: (10, {}), {1}: (11, {})} | custom-call | flops 154828800 | bytes 1474560 | tf_op jit(solution)/shard_map/final/pallas_call | solution.py:289
  78.2 1.4 %final.15 = (f32[60,32,128]{2,1,0:T(8,128)}, f32[60,32,128]{2,1,0:T(8,128)}) custom-call(f32[7,32,128]{2,1,0:T(8,128)S(1)} %bitcast.46, f32[32,128]{1,0:T(8,128)S(1)} %bitcast.55, f32[32,128]{1,0:T(8,128)S(1)} %bitcast.64, s32[32,128]{1,0:T(8,128)S(1)} %bitcast.73, ...), custom_call_target="tpu_custom_call", output_to_operand_aliasing={{0}: (10, {}), {1}: (11, {})} | custom-call | flops 154828800 | bytes 1474560 | tf_op jit(solution)/shard_map/final/pallas_call | solution.py:289
  (61 shorter events, 14.5 us)
Async XLA Ops:
  1.6 16.4 %collective-permute-start = (f32[60,32,128]{2,1,0:T(8,128)}, f32[60,32,128]{2,1,0:T(8,128)S(1)}, u32[]{:S(2)}, u32[]{:S(2)}) collective-permute-start(f32[60,32,128]{2,1,0:T(8,128)} %bitcast.78), channel_id=1, source_target_pairs={{0,2},{2,0},{4,6},{6,4},{8,10},{10,8},{12,14},{14,12},{16,18},{18,... | collective-permute-start | bytes 2949128 | tf_op jit(solution)/shard_map/ppermute | solution.py:325
  1.7 16.4 %collective-permute-start.6 = (f32[480,128]{1,0:T(8,128)S(1)}, f32[480,128]{1,0:T(8,128)S(1)}, u32[]{:S(2)}, u32[]{:S(2)}) collective-permute-start(f32[480,128]{1,0:T(8,128)S(1)} %slice_bitcast_fusion.nxt.cur.refs_6_.prev), channel_id=1, source_target_pairs={{0,30},{2,4},{4,2},{6,8},{8,6},{10,12},{12,10},{14,16},{16,14},{18... | collective-permute-start | bytes 737288 | tf_op jit(solution)/shard_map/ppermute | solution.py:331
  5.6 15.1 %collective-permute-start.4 = (f32[480,128]{1,0:T(8,128)S(1)}, f32[480,128]{1,0:T(8,128)S(1)}, u32[]{:S(2)}, u32[]{:S(2)}) collective-permute-start(f32[480,128]{1,0:T(8,128)S(1)} %get-tuple-element.25.prev.cur.refs_6_.nxt), channel_id=1, source_target_pairs={{0,30},{2,4},{4,2},{6,8},{8,6},{10,12},{12,10},{14,16},{16,14},{18... | collective-permute-start | bytes 737288 | tf_op jit(solution)/shard_map/ppermute | solution.py:331
  5.7 18.9 %collective-permute-start.10 = (f32[480,128]{1,0:T(8,128)S(1)}, f32[480,128]{1,0:T(8,128)S(1)}, u32[]{:S(2)}, u32[]{:S(2)}) collective-permute-start(f32[480,128]{1,0:T(8,128)S(1)} %get-tuple-element.24.prev.nxt.cur.refs_6_), channel_id=1, source_target_pairs={{0,30},{2,4},{4,2},{6,8},{8,6},{10,12},{12,10},{14,16},{16,14},{18... | collective-permute-start | bytes 737288 | tf_op jit(solution)/shard_map/ppermute | solution.py:331
  7.4 21.1 %collective-permute-start.1 = (f32[480,128]{1,0:T(8,128)S(1)}, f32[480,128]{1,0:T(8,128)}, u32[]{:S(2)}, u32[]{:S(2)}) collective-permute-start(f32[480,128]{1,0:T(8,128)S(1)} %get-tuple-element.26.cur.field.refs_6_.nxt.prev), channel_id=1, source_target_pairs={{0,30},{2,4},{4,2},{6,8},{8,6},{10,12},{12,10},{14,16},{16,14},{18... | collective-permute-start | bytes 737288 | tf_op jit(solution)/shard_map/ppermute | solution.py:331
  18.9 13.5 %collective-permute-start.7 = (f32[480,128]{1,0:T(8,128)}, f32[480,128]{1,0:T(8,128)}, u32[]{:S(2)}, u32[]{:S(2)}) collective-permute-start(f32[480,128]{1,0:T(8,128)} %lap.11.refs_7_), channel_id=1, source_target_pairs={{0,1},{1,0},{2,3},{3,2},{4,5},{5,4},{6,7},{7,6},{8,9},{9,8},{10,11... | collective-permute-start | bytes 737288 | tf_op jit(solution)/shard_map/ppermute | solution.py:339
  20.9 5.6 %copy-start = (f32[60,1,32,128]{3,2,1,0:T(8,128)S(1)}, f32[60,1,32,128]{3,2,1,0:T(8,128)}, u32[]{:S(2)}) copy-start(f32[60,1,32,128]{3,2,1,0:T(8,128)} %param.9) | copy-start | bytes 2949124
  20.9 13.4 %collective-permute-start.5 = (f32[480,128]{1,0:T(8,128)S(1)}, f32[480,128]{1,0:T(8,128)}, u32[]{:S(2)}, u32[]{:S(2)}) collective-permute-start(f32[480,128]{1,0:T(8,128)S(1)} %lap.10.refs_7_), channel_id=1, source_target_pairs={{0,1},{1,0},{2,3},{3,2},{4,5},{5,4},{6,7},{7,6},{8,9},{9,8},{10,11... | collective-permute-start | bytes 737288 | tf_op jit(solution)/shard_map/ppermute | solution.py:339
  24.6 1.9 %copy-start.4 = (s32[1,32,128]{2,1,0:T(8,128)S(1)}, s32[1,32,128]{2,1,0:T(8,128)}, u32[]{:S(2)}) copy-start(s32[1,32,128]{2,1,0:T(8,128)} %param.12) | copy-start | bytes 49156
  24.8 12.9 %collective-permute-start.11 = (f32[480,128]{1,0:T(8,128)S(1)}, f32[480,128]{1,0:T(8,128)}, u32[]{:S(2)}, u32[]{:S(2)}) collective-permute-start(f32[480,128]{1,0:T(8,128)S(1)} %lap.13.refs_7_), channel_id=1, source_target_pairs={{0,1},{1,0},{2,3},{3,2},{4,5},{5,4},{6,7},{7,6},{8,9},{9,8},{10,11... | collective-permute-start | bytes 737288 | tf_op jit(solution)/shard_map/ppermute | solution.py:339
  27.2 16.8 %collective-permute-start.3 = (f32[480,128]{1,0:T(8,128)}, f32[480,128]{1,0:T(8,128)}, u32[]{:S(2)}, u32[]{:S(2)}) collective-permute-start(f32[480,128]{1,0:T(8,128)} %blend.1), channel_id=1, source_target_pairs={{0,1},{1,0},{2,3},{3,2},{4,5},{5,4},{6,7},{7,6},{8,9},{9,8},{10,11... | collective-permute-start | bytes 737288 | tf_op jit(solution)/shard_map/ppermute | solution.py:339
  28.5 2.0 %copy-start.1 = (f32[7,1,32,128]{3,2,1,0:T(8,128)S(1)}, f32[7,1,32,128]{3,2,1,0:T(8,128)}, u32[]{:S(2)}) copy-start(f32[7,1,32,128]{3,2,1,0:T(8,128)} %param.13) | copy-start | bytes 344068
  29.7 14.7 %collective-permute-start.2 = (f32[480,128]{1,0:T(8,128)S(1)}, f32[480,128]{1,0:T(8,128)S(1)}, u32[]{:S(2)}, u32[]{:S(2)}) collective-permute-start(f32[480,128]{1,0:T(8,128)S(1)} %lap.9.refs_7_), channel_id=1, source_target_pairs={{0,1},{1,0},{2,3},{3,2},{4,5},{5,4},{6,7},{7,6},{8,9},{9,8},{10,11... | collective-permute-start | bytes 737288 | tf_op jit(solution)/shard_map/ppermute | solution.py:339
  34.2 14.0 %collective-permute-start.15 = (f32[480,128]{1,0:T(8,128)S(1)}, f32[480,128]{1,0:T(8,128)S(1)}, u32[]{:S(2)}, u32[]{:S(2)}) collective-permute-start(f32[480,128]{1,0:T(8,128)S(1)} %final.10.nxt.cur.prev.refs_6_), channel_id=1, source_target_pairs={{0,2},{2,0},{4,6},{6,4},{8,10},{10,8},{12,14},{14,12},{16,18},{18,... | collective-permute-start | bytes 737288 | tf_op jit(solution)/shard_map/ppermute | solution.py:325
  34.3 14.0 %collective-permute-start.16 = (f32[480,128]{1,0:T(8,128)S(1)}, f32[480,128]{1,0:T(8,128)S(1)}, u32[]{:S(2)}, u32[]{:S(2)}) collective-permute-start(f32[480,128]{1,0:T(8,128)S(1)} %final.10.nxt.cur.prev.refs_6_), channel_id=1, source_target_pairs={{0,30},{2,4},{4,2},{6,8},{8,6},{10,12},{12,10},{14,16},{16,14},{18... | collective-permute-start | bytes 737288 | tf_op jit(solution)/shard_map/ppermute | solution.py:331
  37.7 10.7 %collective-permute-start.12 = (f32[480,128]{1,0:T(8,128)S(1)}, f32[480,128]{1,0:T(8,128)S(1)}, u32[]{:S(2)}, u32[]{:S(2)}) collective-permute-start(f32[480,128]{1,0:T(8,128)S(1)} %final.9.prev.cur.nxt.refs_6_), channel_id=1, source_target_pairs={{0,2},{2,0},{4,6},{6,4},{8,10},{10,8},{12,14},{14,12},{16,18},{18,... | collective-permute-start | bytes 737288 | tf_op jit(solution)/shard_map/ppermute | solution.py:325
  44.0 8.3 %collective-permute-start.13 = (f32[480,128]{1,0:T(8,128)S(1)}, f32[480,128]{1,0:T(8,128)S(1)}, u32[]{:S(2)}, u32[]{:S(2)}) collective-permute-start(f32[480,128]{1,0:T(8,128)S(1)} %final.9.prev.cur.nxt.refs_6_), channel_id=1, source_target_pairs={{0,30},{2,4},{4,2},{6,8},{8,6},{10,12},{12,10},{14,16},{16,14},{18... | collective-permute-start | bytes 737288 | tf_op jit(solution)/shard_map/ppermute | solution.py:331
  44.4 8.6 %collective-permute-start.18 = (f32[480,128]{1,0:T(8,128)S(1)}, f32[480,128]{1,0:T(8,128)S(1)}, u32[]{:S(2)}, u32[]{:S(2)}) collective-permute-start(f32[480,128]{1,0:T(8,128)S(1)} %final.11.prev.nxt.cur.refs_6_), channel_id=1, source_target_pairs={{0,2},{2,0},{4,6},{6,4},{8,10},{10,8},{12,14},{14,12},{16,18},{18,... | collective-permute-start | bytes 737288 | tf_op jit(solution)/shard_map/ppermute | solution.py:325
  48.2 22.5 %collective-permute-start.8 = (f32[960,128]{1,0:T(8,128)S(1)}, f32[960,128]{1,0:T(8,128)S(1)}, u32[]{:S(2)}, u32[]{:S(2)}) collective-permute-start(f32[960,128]{1,0:T(8,128)S(1)} %final.8.cur.nxt.prev.refs_6_), channel_id=1, source_target_pairs={{0,2},{2,0},{4,6},{6,4},{8,10},{10,8},{12,14},{14,12},{16,18},{18,... | collective-permute-start | bytes 1474568 | tf_op jit(solution)/shard_map/ppermute | solution.py:325
  48.3 22.4 %collective-permute-start.9 = (f32[960,128]{1,0:T(8,128)S(1)}, f32[960,128]{1,0:T(8,128)S(1)}, u32[]{:S(2)}, u32[]{:S(2)}) collective-permute-start(f32[960,128]{1,0:T(8,128)S(1)} %final.8.cur.nxt.prev.refs_6_), channel_id=1, source_target_pairs={{0,30},{2,4},{4,2},{6,8},{8,6},{10,12},{12,10},{14,16},{16,14},{18... | collective-permute-start | bytes 1474568 | tf_op jit(solution)/shard_map/ppermute | solution.py:331
  48.4 20.1 %collective-permute-start.19 = (f32[480,128]{1,0:T(8,128)S(1)}, f32[480,128]{1,0:T(8,128)S(1)}, u32[]{:S(2)}, u32[]{:S(2)}) collective-permute-start(f32[480,128]{1,0:T(8,128)S(1)} %final.11.prev.nxt.cur.refs_6_), channel_id=1, source_target_pairs={{0,30},{2,4},{4,2},{6,8},{8,6},{10,12},{12,10},{14,16},{16,14},{18... | collective-permute-start | bytes 737288 | tf_op jit(solution)/shard_map/ppermute | solution.py:331
  52.4 22.8 %collective-permute-start.17 = (f32[540,128]{1,0:T(8,128)S(1)}, f32[540,128]{1,0:T(8,128)S(1)}, u32[]{:S(2)}, u32[]{:S(2)}) collective-permute-start(f32[540,128]{1,0:T(8,128)S(1)} %lap.15.refs_7_), channel_id=1, source_target_pairs={{0,1},{1,0},{2,3},{3,2},{4,5},{5,4},{6,7},{7,6},{8,9},{9,8},{10,11... | collective-permute-start | bytes 829448 | tf_op jit(solution)/shard_map/ppermute | solution.py:339
  53.0 22.2 %collective-permute-start.14 = (f32[540,128]{1,0:T(8,128)S(1)}, f32[540,128]{1,0:T(8,128)S(1)}, u32[]{:S(2)}, u32[]{:S(2)}) collective-permute-start(f32[540,128]{1,0:T(8,128)S(1)} %lap.14.refs_7_), channel_id=1, source_target_pairs={{0,1},{1,0},{2,3},{3,2},{4,5},{5,4},{6,7},{7,6},{8,9},{9,8},{10,11... | collective-permute-start | bytes 829448 | tf_op jit(solution)/shard_map/ppermute | solution.py:339
  68.7 5.1 %collective-permute-start.20 = (f32[480,128]{1,0:T(8,128)S(1)}, f32[480,128]{1,0:T(8,128)S(1)}, u32[]{:S(2)}, u32[]{:S(2)}) collective-permute-start(f32[480,128]{1,0:T(8,128)S(1)} %lap.17.refs_7_), channel_id=1, source_target_pairs={{0,1},{1,0},{2,3},{3,2},{4,5},{5,4},{6,7},{7,6},{8,9},{9,8},{10,11... | collective-permute-start | bytes 737288 | tf_op jit(solution)/shard_map/ppermute | solution.py:339
  (4 other events, 5.7 us)
where the time goes:
time: 80 us; the launch traced here: 79.6 us
  waiting for transfers between devices  32.6 us (41%)
  Pallas kernels  22.4 us (28%)
  starting transfers between devices  21.2 us (26%)
  local copies, waits for them, and re-layouts  2.47 us (3%)
  between operations  0.93 us (1%)
    ppermute x8, waiting for transfers between devices, far_swap(): return lax.ppermute(x, 'space', pairs)  29.9 us
    pallas_call x8, Pallas kernels, final_call(): pl.pallas_call(functools.partial(final_kernel, n, chunk, field[1], len(la...  12.4 us
    ppermute x8, starting transfers between devices, far_swap(): return lax.ppermute(x, 'space', pairs)  8.16 us
    ppermute x8, starting transfers between devices, to_others(): got.append(lax.ppermute(x, 'modes', ring))  7.45 us
    ppermute x5, starting transfers between devices, near_swap(): return lax.ppermute(x, 'space', [(i, i ^ 1) for i in range(count)])  5.55 us
    pallas_call x8, Pallas kernels, own_call(): pl.pallas_call(functools.partial(own_kernel, n, chunk, blocks), out_shape...  5.26 us
    pallas_call x9, Pallas kernels, lap_call(): pl.pallas_call(functools.partial(lap_kernel, n, chunk, slots, edge, compa...  3.43 us
    ppermute x8, waiting for transfers between devices, to_others(): got.append(lax.ppermute(x, 'modes', ring))  2.72 us
  transfers between devices with their start and end apart: 21, of which 8 were waited for; matrix products, arithmetic and copies ran while one was open for 2% of the time, Pallas kernels for 23%

commit v1 on v0

--- a/solution.py
+++ b/solution.py
@@ -46,13 +46,13 @@
         def take(ref, slot):
             return ref[pl.ds((slot * n + j) * ROWS, g * ROWS), :].reshape(g, ROWS, nz)
 
-        def handed(ref):
-            rows = [ref[pl.ds(n * ROWS + j + i, 1), :] for i in range(g)]
+        def handed(ref, at):
+            rows = [ref[pl.ds(at + j + i, 1), :] for i in range(g)]
             return jnp.stack([jnp.broadcast_to(r, (ROWS, nz)) for r in rows])
 
         x = take(cur, slots[1])
         if compact:
-            before, after = handed(prev), handed(nxt)
+            before, after = handed(prev, n * ROWS), handed(nxt, n * ROWS + ceil_to(n, 8))
         else:
             before = pltpu.roll(take(prev, slots[0]), 1, 1)
             after = pltpu.roll(take(nxt, slots[2]), ROWS - 1, 1)
@@ -65,9 +65,10 @@
         sides = pltpu.roll(x, 1, 2) + pltpu.roll(x, nz - 1, 2)
         beside = (up + down) + sides + (inside + take(far, slots[4]))
         out[pl.ds(j * ROWS, g * ROWS), :] = (6.0 * x - beside).reshape(g * ROWS, nz)
-    if edge is not None:
-        start = slots[1] * n * ROWS + edge
-        out[pl.ds(n * ROWS, n), :] = cur[pl.ds(start, n, stride=ROWS), :]
+    if edge:
+        for i, (ref, slot, y) in enumerate(((nxt, slots[2], ROWS - 1), (prev, slots[0], 0))):
+            got = ref[pl.ds(slot * n * ROWS + y, n, stride=ROWS), :]
+            out[pl.ds(n * ROWS + i * ceil_to(n, 8), n), :] = got
 
 
 def couple(n, chunk, blocks, fields, matrix, lap, rhs, mixed, emit):
@@ -124,44 +125,61 @@
         out[rows, :] = v.reshape(g * ROWS, nz)
 
 
-def final_kernel(n, chunk, slot, others, last, double, *refs):
-    fields, slope, average, metal, matrices, source, field, lap, own = refs[:9]
-    laps, refs = refs[9 : 9 + others], refs[9 + others :]
+def final_kernel(n, entries, last, double, *refs):
+    fields, slope, average, metal, matrices, source = refs[:6]
+    refs = refs[6:]
+    groups = []
+    for chunk, slot, has_own, others in entries:
+        size = 2 + has_own + others
+        groups.append((chunk, slot, has_own, refs[:size]))
+        refs = refs[size:]
     blended, refs = (refs[0], refs[1:]) if double else (None, refs)
     outs, (rhs, mixed, sums) = refs[:-3], refs[-3:]
     outs = outs[2:] if len(outs) == 4 else outs
-    nz = lap.shape[1]
     clear_rhs(n, rhs)
-    for other in range(others):
-        base = own if other == 0 else sums
-
-        def emit(y, b, total):
-            at = pl.ds(b * n * ROWS + y, n, stride=ROWS)
-            sums[at, :] = base[at, :] + total
-
-        blocks = 2 if double else 1
-        couple(
-            n, chunk, blocks, fields, matrices.at[1 + other], laps[other], rhs, mixed, emit
-        )
-    here, cond, step = cell_factors(chunk, slope, average, metal)
     g = group_of(n)
-    for j in range(0, n, g):
-
-        def take(ref, part=0):
-            rows = pl.ds((part * n + j) * ROWS, g * ROWS)
-            return ref[rows, :].reshape(g, ROWS, nz)
-
-        u = take(field, slot)
-        residual = source[pl.ds(j, g)] - (here * u + (cond * take(lap) + take(sums)))
-        u = u + step * residual
-        if last:
-            outs[0][pl.ds(j, g)] = u
-            outs[1][pl.ds(j, g)] = residual
-        else:
-            outs[0][pl.ds(j * ROWS, g * ROWS), :] = u.reshape(g * ROWS, nz)
-        if double:
-            u = take(blended) - step * (cond * take(laps[0]) + take(sums, 1))
-            outs[0][pl.ds((n + j) * ROWS, g * ROWS), :] = u.reshape(g * ROWS, nz)
+    for index, (chunk, slot, has_own, (field, lap, *laps)) in enumerate(groups):
+        nz = lap.shape[1]
+        base = laps[0] if has_own else None
+        laps = laps[1:] if has_own else [lap, *laps]
+        for other, received in enumerate(laps):
+
+            def emit(y, b, total):
+                at = pl.ds(b * n * ROWS + y, n, stride=ROWS)
+                sums[at, :] = total if base is None else base[at, :] + total
+
+            couple(
+                n,
+                chunk,
+                2 if double else 1,
+                fields,
+                matrices.at[other + has_own],
+                received,
+                rhs,
+                mixed,
+                emit,
+            )
+            base = sums
+        here, cond, step = cell_factors(chunk, slope, average, metal)
+        rows_here = pl.ds(index * ROWS, ROWS)
+        for j in range(0, n, g):
+
+            def take(ref, part=0):
+                rows = pl.ds((part * n + j) * ROWS, g * ROWS)
+                return ref[rows, :].reshape(g, ROWS, nz)
+
+            u = take(field, slot)
+            rest = here * u + (cond * take(lap) + take(sums))
+            residual = source[pl.ds(j, g), rows_here, :] - rest
+            u = u + step * residual
+            if last:
+                outs[0][pl.ds(j, g), rows_here, :] = u
+                outs[1][pl.ds(j, g), rows_here, :] = residual
+            else:
+                outs[0][pl.ds(j * ROWS, g * ROWS), :] = u.reshape(g * ROWS, nz)
+            if double:
+                u = take(blended) - step * (cond * take(laps[0]) + take(sums, 1))
+                outs[0][pl.ds((n + j) * ROWS, g * ROWS), :] = u.reshape(g * ROWS, nz)
 
 
 def matrices_kernel(n, count, blocks, me, pairs, entries, out):
@@ -220,10 +238,10 @@
     ]
 
 
-def lap_call(n, chunk, prev, cur, nxt, near, far, edge=None, compact=False):
+def lap_call(n, chunk, prev, cur, nxt, near, far, edge=False, compact=False):
     arrays, slots = zip(prev, cur, nxt, near, far)
     nz = cur[0].shape[1]
-    rows = n * ROWS + (0 if edge is None else n)
+    rows = n * ROWS + (2 * ceil_to(n, 8) if edge else 0)
     return pl.pallas_call(
         functools.partial(lap_kernel, n, chunk, slots, edge, compact),
         out_shape=jax.ShapeDtypeStruct((rows, nz), F32),
@@ -266,17 +284,23 @@
     )(*operands)
 
 
-def final_call(n, chunk, last, shared, matrices, source, field, lap, own, laps, blended, outs):
+def final_call(n, chunks, last, shared, matrices, source, parts, blended, outs):
     nz = source.shape[2]
     double = blended is not None
     blocks = 2 if double else 1
-    operands = [*shared, matrices, source, field[0], lap, own, *laps]
+    block = pl.BlockSpec(
+        (n, len(chunks) * ROWS, nz), lambda i: (0, chunks[0] // len(chunks), 0)
+    )
+    operands, entries = [*shared, matrices, source], []
+    for chunk, (field, lap, own, laps) in zip(chunks, parts):
+        entries.append((chunk, field[1], own is not None, len(laps)))
+        operands += [field[0], lap, *([] if own is None else [own]), *laps]
     operands += [blended] if double else []
-    specs = [rows_of(a, chunk) if a is source else whole(a) for a in operands]
+    specs = [block if a is source else whole(a) for a in operands]
     aliases = {}
     if last:
         shapes = [jax.ShapeDtypeStruct(source.shape, F32)] * 2
-        out_specs = [rows_of(source, chunk)] * 2
+        out_specs = [block] * 2
         if outs:
             aliases = {len(operands) + i: i for i in range(2)}
             operands += list(outs)
@@ -284,10 +308,10 @@
     else:
         shapes = [jax.ShapeDtypeStruct((blocks * n * ROWS, nz), F32)]
         out_specs = [whole(shapes[0])]
-    size = n * ROWS * nz
+    size = len(chunks) * n * ROWS * nz
     kl = shared[0].shape[0]
     return pl.pallas_call(
-        functools.partial(final_kernel, n, chunk, field[1], len(laps), last, double),
+        functools.partial(final_kernel, n, tuple(entries), last, double),
         grid=(1,),
         out_shape=shapes,
         in_specs=specs,
@@ -299,7 +323,7 @@
         input_output_aliases=aliases,
         compiler_params=params(),
         name="final",
-        cost_estimate=estimate(6 * blocks * len(laps) * kl * n * size, 6 * size),
+        cost_estimate=estimate(6 * blocks * kl * n * size, 6 * size),
     )(*operands)
 
 
@@ -340,7 +364,7 @@
     return got
 
 
-FINALS = (1, 0, 2, 3)
+FINALS = ((1,), (0,), (2, 3))
 
 
 def doubled(count, devices):
@@ -376,20 +400,18 @@
         for c in range(count):
             both = double and c == tail
             prev, nxt = field[(c - 1) % count], field[(c + 1) % count]
-            edge = None
-            if double and last and not both:
-                edge = {(tail - 1): ROWS - 1, (tail + 1) % count: 0}.get(c)
+            edge = double and last and c == tail - 2
             lap = lap_call(n, c, prev, field[c], nxt, near[c], far[c], edge)
             if both and last:
                 of_other = lambda a: (a[0], 1)
-                handed = [(parts[d % count][3][0], 0) for d in (tail - 1, tail + 1)]
+                handed = (parts[tail - 2][3][0], 0)
                 laps = [
                     lap_call(
                         n,
                         c,
-                        handed[0],
+                        handed,
                         of_other(field[c]),
-                        handed[1],
+                        handed,
                         of_other(near[c]),
                         of_other(far[c]),
                         compact=True,
@@ -397,14 +419,25 @@
                 ]
             else:
                 laps = to_others(lap)
-            blocks = 2 if both and not last else 1
-            own = own_call(n, c, blocks, shared[0], matrices, lap)
+            own = None
+            if not (both and last):
+                blocks = 2 if both else 1
+                own = own_call(n, c, blocks, shared[0], matrices, lap)
             parts[c] = (field[c], lap, own, laps)
         new = {}
-        for c in FINALS if last and double else range(count):
+        for chunks in FINALS if last and double else [(c,) for c in range(count)]:
+            c = chunks[0]
             given = blended if double and c == tail and not last else None
             got = final_call(
-                n, c, last, shared, matrices, source, *parts[c], given, outs
+                n,
+                chunks,
+                last,
+                shared,
+                matrices,
+                source,
+                [parts[d] for d in chunks],
+                given,
+                outs,
             )
             if last:
                 outs = got

time: 80 us -> 75.3 us (0.941)
  waiting for transfers between devices: 32.6 us -> 29 us
  Pallas kernels: 22.4 us -> 20.5 us
  starting transfers between devices: 21.2 us -> 22.4 us
    ppermute x8, waiting for transfers between devices: 29.9 us -> 27.4 us  [far_swap(): return lax.ppermute(x, 'space', pairs)]
    ppermute x8, starting transfers between devices: 7.45 us -> 9.66 us  [to_others(): got.append(lax.ppermute(x, 'modes', ring))]
    ppermute x8, starting transfers between devices: 8.16 us -> 6.18 us  [far_swap(): return lax.ppermute(x, 'space', pairs)]
    pallas_call x8 -> x7, Pallas kernels: 12.4 us -> 11 us  [final_call(): pl.pallas_call(functools.partial(final_kernel, n, tuple(entries), last, d...]
    ppermute x8, waiting for transfers between devices: 2.72 us -> 1.52 us  [to_others(): got.append(lax.ppermute(x, 'modes', ring))]
    ppermute x5, starting transfers between devices: 5.55 us -> 6.52 us  [near_swap(): return lax.ppermute(x, 'space', [(i, i ^ 1) for i in range(count)])]
    pallas_call x8 -> x7, Pallas kernels: 5.26 us -> 4.76 us  [own_call(): pl.pallas_call(functools.partial(own_kernel, n, chunk, blocks), out_shape...]
  transfers between devices with their start and end apart: 21 -> 21, of which waited for: 8 -> 5; matrix products, arithmetic and copies ran while one was open for 2% -> 2% of each run, Pallas kernels for 23% -> 24%
where the time goes in v1:
time: 75.3 us; the launch traced here: 74.9 us
  waiting for transfers between devices  29 us (39%)
  starting transfers between devices  22.4 us (30%)
  Pallas kernels  20.5 us (27%)
  local copies, waits for them, and re-layouts  2.23 us (3%)
  between operations  0.91 us (1%)
    ppermute x8, waiting for transfers between devices, far_swap(): return lax.ppermute(x, 'space', pairs)  27.4 us
    pallas_call x7, Pallas kernels, final_call(): pl.pallas_call(functools.partial(final_kernel, n, tuple(entries), last, d...  11 us
    ppermute x8, starting transfers between devices, to_others(): got.append(lax.ppermute(x, 'modes', ring))  9.66 us
    ppermute x5, starting transfers between devices, near_swap(): return lax.ppermute(x, 'space', [(i, i ^ 1) for i in range(count)])  6.52 us
    ppermute x8, starting transfers between devices, far_swap(): return lax.ppermute(x, 'space', pairs)  6.18 us
    pallas_call x7, Pallas kernels, own_call(): pl.pallas_call(functools.partial(own_kernel, n, chunk, blocks), out_shape...  4.76 us
    pallas_call x9, Pallas kernels, lap_call(): pl.pallas_call(functools.partial(lap_kernel, n, chunk, slots, edge, compa...  3.43 us
    reshape x2, local copies, waits for them, and re-layouts, rounds(): cut = lambda c: u0[:, c * ROWS:(c + 1) * ROWS].reshape(n * ROWS, nz)  2.2 us
  transfers between devices with their start and end apart: 21, of which 5 were waited for; matrix products, arithmetic and copies ran while one was open for 2% of the time, Pallas kernels for 24%

profile of v1, /device:TPU:1, one launch (start us, length us, event | category | flops | bytes accessed | tf_op | source)
XLA Modules:
  0.0 74.9 jit_solution(15895704040411956272)
XLA Ops:
  1.7 1.2 %slice_bitcast_fusion.1 = (f32[480,128]{1,0:T(8,128)S(1)}, f32[480,128]{1,0:T(8,128)S(1)}, f32[480,128]{1,0:T(8,128)S(1)}) fusion(f32[60,32,128]{2,1,0:T(8,128)} %bitcast.73), kind=kLoop, calls=%fused_computation.1 | loop fusion | bytes 1474560 | tf_op jit(solution)/shard_map/reshape | solution.py:378
  2.9 2.7 %collective-permute-start.3 = (f32[480,128]{1,0:T(8,128)S(1)}, f32[480,128]{1,0:T(8,128)S(1)}, u32[]{:S(2)}, u32[]{:S(2)}) collective-permute-start(f32[480,128]{1,0:T(8,128)S(1)} %get-tuple-element.21.prev.cur.refs_6_.nxt), channel_id=1, source_target_pairs={{0,30},{2,4},{4,2},{6,8},{8,6},{10,12},{12,10},{14,16},{16,14},{18... | collective-permute-start | bytes 737288 | tf_op jit(solution)/shard_map/ppermute | solution.py:355
  5.7 1.7 %collective-permute-start.5 = (f32[480,128]{1,0:T(8,128)S(1)}, f32[480,128]{1,0:T(8,128)S(1)}, u32[]{:S(2)}, u32[]{:S(2)}) collective-permute-start(f32[480,128]{1,0:T(8,128)S(1)} %get-tuple-element.20.nxt.cur.field.refs_6_.prev), channel_id=1, source_target_pairs={{0,30},{2,4},{4,2},{6,8},{8,6},{10,12},{12,10},{14,16},{16,14},{18... | collective-permute-start | bytes 737288 | tf_op jit(solution)/shard_map/ppermute | solution.py:355
  7.4 11.8 %collective-permute-done.3.far = f32[480,128]{1,0:T(8,128)S(1)} collective-permute-done((f32[480,128]{1,0:T(8,128)S(1)}, f32[480,128]{1,0:T(8,128)S(1)}, u32[]{:S(2)}, u32[]{:S(2)}) %collective-permute-start.3) | collective-permute-done | bytes 245792 | tf_op jit(solution)/shard_map/ppermute | solution.py:355
  20.2 1.2 %collective-permute-start.4 = (f32[480,128]{1,0:T(8,128)}, f32[480,128]{1,0:T(8,128)}, u32[]{:S(2)}, u32[]{:S(2)}) collective-permute-start(f32[480,128]{1,0:T(8,128)} %lap.10.refs_7_), channel_id=1, source_target_pairs={{0,1},{1,0},{2,3},{3,2},{4,5},{5,4},{6,7},{7,6},{8,9},{9,8},{10,11... | collective-permute-start | bytes 737288 | tf_op jit(solution)/shard_map/ppermute | solution.py:363
  21.4 1.7 %collective-permute-done.11.far = f32[480,128]{1,0:T(8,128)S(1)} collective-permute-done((f32[480,128]{1,0:T(8,128)S(1)}, f32[480,128]{1,0:T(8,128)S(1)}, u32[]{:S(2)}, u32[]{:S(2)}) %collective-permute-start.11) | collective-permute-done | bytes 245792 | tf_op jit(solution)/shard_map/ppermute | solution.py:355
  23.3 1.9 %collective-permute-start.12 = (f32[480,128]{1,0:T(8,128)S(1)}, f32[480,128]{1,0:T(8,128)}, u32[]{:S(2)}, u32[]{:S(2)}) collective-permute-start(f32[480,128]{1,0:T(8,128)S(1)} %lap.13.refs_7_), channel_id=1, source_target_pairs={{0,1},{1,0},{2,3},{3,2},{4,5},{5,4},{6,7},{7,6},{8,9},{9,8},{10,11... | collective-permute-start | bytes 737288 | tf_op jit(solution)/shard_map/ppermute | solution.py:363
  26.6 1.2 %collective-permute-start.6 = (f32[480,128]{1,0:T(8,128)S(1)}, f32[480,128]{1,0:T(8,128)}, u32[]{:S(2)}, u32[]{:S(2)}) collective-permute-start(f32[480,128]{1,0:T(8,128)S(1)} %lap.11.refs_7_), channel_id=1, source_target_pairs={{0,1},{1,0},{2,3},{3,2},{4,5},{5,4},{6,7},{7,6},{8,9},{9,8},{10,11... | collective-permute-start | bytes 737288 | tf_op jit(solution)/shard_map/ppermute | solution.py:363
  28.3 1.2 %lap.9.refs_7_ = f32[480,128]{1,0:T(8,128)S(1)} custom-call(f32[480,128]{1,0:T(8,128)S(1)} %get-tuple-element.21.prev.cur.refs_6_.nxt, f32[480,128]{1,0:T(8,128)S(1)} %get-tuple-element.22.cur.refs_6_.nxt.prev, f32[480,128]{1,0:T(8,128)S(1)} %get-tuple-element.20.nxt.cur.field.refs_6_.prev, f32[60,32,128]{2,1,0:T(8,128)S(1)} %collective-permute-done.near, ...), custom_call_target="tpu_custom_call" | custom-call | flops 737280 | bytes 1474560 | tf_op jit(solution)/shard_map/lap/pallas_call | solution.py:245
  29.5 1.8 %collective-permute-start.2 = (f32[480,128]{1,0:T(8,128)S(1)}, f32[480,128]{1,0:T(8,128)S(1)}, u32[]{:S(2)}, u32[]{:S(2)}) collective-permute-start(f32[480,128]{1,0:T(8,128)S(1)} %lap.9.refs_7_), channel_id=1, source_target_pairs={{0,1},{1,0},{2,3},{3,2},{4,5},{5,4},{6,7},{7,6},{8,9},{9,8},{10,11... | collective-permute-start | bytes 737288 | tf_op jit(solution)/shard_map/ppermute | solution.py:363
  31.3 1.5 %own.8.refs_8_ = f32[480,128]{1,0:T(8,128)S(1)} custom-call(f32[7,32,128]{2,1,0:T(8,128)S(1)} %bitcast.30, bf16[2,896,192]{2,1,0:T(8,128)(2,1)S(1)} %coupling.1.matrices.refs_4_, f32[480,128]{1,0:T(8,128)} %lap.10.refs_7_), custom_call_target="tpu_custom_call" | custom-call | flops 154828800 | bytes 491520 | tf_op jit(solution)/shard_map/own/pallas_call | solution.py:259
  32.8 1.7 %final.8.prev.cur.nxt.refs_6_ = f32[480,128]{1,0:T(8,128)S(1)} custom-call(f32[7,32,128]{2,1,0:T(8,128)S(1)} %bitcast.31, f32[32,128]{1,0:T(8,128)S(1)} %bitcast.45, f32[32,128]{1,0:T(8,128)S(1)} %bitcast.53, s32[32,128]{1,0:T(8,128)S(1)} %bitcast.61, bf16[2,896,192]{2,1,0:T(8,128)(2,1)S(1)} %coupling.1.matrices.refs_4_, f32[60,32,128]{2,1,0:T(8,128)S(1)} %bitcast.23, ...), custom_call_target="tpu_custom_call" | custom-call | flops 154828800 | bytes 1474560 | tf_op jit(solution)/shard_map/final/pallas_call | solution.py:313
  35.1 1.2 %collective-permute-start.16 = (f32[480,128]{1,0:T(8,128)S(1)}, f32[480,128]{1,0:T(8,128)S(1)}, u32[]{:S(2)}, u32[]{:S(2)}) collective-permute-start(f32[480,128]{1,0:T(8,128)S(1)} %final.8.prev.cur.nxt.refs_6_), channel_id=1, source_target_pairs={{0,30},{2,4},{4,2},{6,8},{8,6},{10,12},{12,10},{14,16},{16,14},{18... | collective-permute-start | bytes 737288 | tf_op jit(solution)/shard_map/ppermute | solution.py:355
  36.3 1.6 %final.10.nxt.prev.cur.refs_6_ = f32[480,128]{1,0:T(8,128)S(1)} custom-call(f32[7,32,128]{2,1,0:T(8,128)S(1)} %bitcast.33, f32[32,128]{1,0:T(8,128)S(1)} %bitcast.46, f32[32,128]{1,0:T(8,128)S(1)} %bitcast.54, s32[32,128]{1,0:T(8,128)S(1)} %bitcast.62, bf16[2,896,192]{2,1,0:T(8,128)(2,1)S(1)} %coupling.1.matrices.refs_4_, f32[60,32,128]{2,1,0:T(8,128)S(1)} %bitcast.24, ...), custom_call_target="tpu_custom_call" | custom-call | flops 154828800 | bytes 1474560 | tf_op jit(solution)/shard_map/final/pallas_call | solution.py:313
  38.9 2.6 %collective-permute-start.18 = (f32[480,128]{1,0:T(8,128)S(1)}, f32[480,128]{1,0:T(8,128)S(1)}, u32[]{:S(2)}, u32[]{:S(2)}) collective-permute-start(f32[480,128]{1,0:T(8,128)S(1)} %final.10.nxt.prev.cur.refs_6_), channel_id=1, source_target_pairs={{0,2},{2,0},{4,6},{6,4},{8,10},{10,8},{12,14},{14,12},{16,18},{18,... | collective-permute-start | bytes 737288 | tf_op jit(solution)/shard_map/ppermute | solution.py:349
  42.8 2.0 %final.9.nxt.cur.prev.refs_10_ = f32[960,128]{1,0:T(8,128)S(1)} custom-call(f32[7,32,128]{2,1,0:T(8,128)S(1)} %bitcast.35, f32[32,128]{1,0:T(8,128)S(1)} %bitcast.47, f32[32,128]{1,0:T(8,128)S(1)} %bitcast.55, s32[32,128]{1,0:T(8,128)S(1)} %bitcast.63, bf16[2,896,192]{2,1,0:T(8,128)(2,1)S(1)} %coupling.1.matrices.refs_4_, f32[60,32,128]{2,1,0:T(8,128)S(1)} %bitcast.25, ...), custom_call_target="tpu_custom_call" | custom-call | flops 309657600 | bytes 1474560 | tf_op jit(solution)/shard_map/final/pallas_call | solution.py:313
  44.9 1.4 %collective-permute-start.13 = (f32[960,128]{1,0:T(8,128)S(1)}, f32[960,128]{1,0:T(8,128)S(1)}, u32[]{:S(2)}, u32[]{:S(2)}) collective-permute-start(f32[960,128]{1,0:T(8,128)S(1)} %final.9.nxt.cur.prev.refs_10_), channel_id=1, source_target_pairs={{0,2},{2,0},{4,6},{6,4},{8,10},{10,8},{12,14},{14,12},{16,18},{18,... | collective-permute-start | bytes 1474568 | tf_op jit(solution)/shard_map/ppermute | solution.py:349
  48.0 2.3 %collective-permute-start.8 = (f32[480,128]{1,0:T(8,128)S(1)}, f32[480,128]{1,0:T(8,128)S(1)}, u32[]{:S(2)}, u32[]{:S(2)}) collective-permute-start(f32[480,128]{1,0:T(8,128)S(1)} %final.7.cur.prev.nxt.refs_6_), channel_id=1, source_target_pairs={{0,2},{2,0},{4,6},{6,4},{8,10},{10,8},{12,14},{14,12},{16,18},{18,... | collective-permute-start | bytes 737288 | tf_op jit(solution)/shard_map/ppermute | solution.py:349
  50.5 1.2 %collective-permute-start.17 = (f32[608,128]{1,0:T(8,128)S(1)}, f32[608,128]{1,0:T(8,128)S(1)}, u32[]{:S(2)}, u32[]{:S(2)}) collective-permute-start(f32[608,128]{1,0:T(8,128)S(1)} %lap.15.refs_7_), channel_id=1, source_target_pairs={{0,1},{1,0},{2,3},{3,2},{4,5},{5,4},{6,7},{7,6},{8,9},{9,8},{10,11... | collective-permute-start | bytes 933896 | tf_op jit(solution)/shard_map/ppermute | solution.py:363
  52.5 13.9 %collective-permute-done.9.far = f32[480,128]{1,0:T(8,128)S(1)} collective-permute-done((f32[480,128]{1,0:T(8,128)S(1)}, f32[480,128]{1,0:T(8,128)S(1)}, u32[]{:S(2)}, u32[]{:S(2)}) %collective-permute-start.9) | collective-permute-done | bytes 245792 | tf_op jit(solution)/shard_map/ppermute | solution.py:355
  66.6 1.3 %collective-permute-start.10 = (f32[480,128]{1,0:T(8,128)S(1)}, f32[480,128]{1,0:T(8,128)S(1)}, u32[]{:S(2)}, u32[]{:S(2)}) collective-permute-start(f32[480,128]{1,0:T(8,128)S(1)} %lap.12.refs_7_), channel_id=1, source_target_pairs={{0,1},{1,0},{2,3},{3,2},{4,5},{5,4},{6,7},{7,6},{8,9},{9,8},{10,11... | collective-permute-start | bytes 737288 | tf_op jit(solution)/shard_map/ppermute | solution.py:363
  69.9 1.4 %final.11 = (f32[60,32,128]{2,1,0:T(8,128)}, f32[60,32,128]{2,1,0:T(8,128)}) custom-call(f32[7,32,128]{2,1,0:T(8,128)S(1)} %bitcast.41, f32[32,128]{1,0:T(8,128)S(1)} %bitcast.49, f32[32,128]{1,0:T(8,128)S(1)} %bitcast.57, s32[32,128]{1,0:T(8,128)S(1)} %bitcast.65, bf16[2,896,192]{2,1,0:T(8,128)(2,1)S(1)} %coupling.1.matrices.refs_4_, ...), custom_call_target="tpu_custom_call" | custom-call | flops 154828800 | bytes 1474560 | tf_op jit(solution)/shard_map/final/pallas_call | solution.py:313
  71.3 1.4 %final.12 = (f32[60,32,128]{2,1,0:T(8,128)}, f32[60,32,128]{2,1,0:T(8,128)}) custom-call(f32[7,32,128]{2,1,0:T(8,128)S(1)} %bitcast.42, f32[32,128]{1,0:T(8,128)S(1)} %bitcast.50, f32[32,128]{1,0:T(8,128)S(1)} %bitcast.58, s32[32,128]{1,0:T(8,128)S(1)} %bitcast.66, ...), custom_call_target="tpu_custom_call", output_to_operand_aliasing={{0}: (10, {}), {1}: (11, {})} | custom-call | flops 154828800 | bytes 1474560 | tf_op jit(solution)/shard_map/final/pallas_call | solution.py:313
  72.7 2.2 %final.13 = (f32[60,32,128]{2,1,0:T(8,128)}, f32[60,32,128]{2,1,0:T(8,128)}) custom-call(f32[7,32,128]{2,1,0:T(8,128)S(1)} %bitcast.43, f32[32,128]{1,0:T(8,128)S(1)} %bitcast.51, f32[32,128]{1,0:T(8,128)S(1)} %bitcast.59, s32[32,128]{1,0:T(8,128)S(1)} %bitcast.67, ...), custom_call_target="tpu_custom_call", output_to_operand_aliasing={{0}: (13, {}), {1}: (14, {})} | custom-call | flops 309657600 | bytes 2949120 | tf_op jit(solution)/shard_map/final/pallas_call | solution.py:313
  (59 shorter events, 11.9 us)
Async XLA Ops:
  1.6 17.7 %collective-permute-start = (f32[60,32,128]{2,1,0:T(8,128)}, f32[60,32,128]{2,1,0:T(8,128)S(1)}, u32[]{:S(2)}, u32[]{:S(2)}) collective-permute-start(f32[60,32,128]{2,1,0:T(8,128)} %bitcast.72), channel_id=1, source_target_pairs={{0,2},{2,0},{4,6},{6,4},{8,10},{10,8},{12,14},{14,12},{16,18},{18,... | collective-permute-start | bytes 2949128 | tf_op jit(solution)/shard_map/ppermute | solution.py:349
  2.9 16.4 %collective-permute-start.3 = (f32[480,128]{1,0:T(8,128)S(1)}, f32[480,128]{1,0:T(8,128)S(1)}, u32[]{:S(2)}, u32[]{:S(2)}) collective-permute-start(f32[480,128]{1,0:T(8,128)S(1)} %get-tuple-element.21.prev.cur.refs_6_.nxt), channel_id=1, source_target_pairs={{0,30},{2,4},{4,2},{6,8},{8,6},{10,12},{12,10},{14,16},{16,14},{18... | collective-permute-start | bytes 737288 | tf_op jit(solution)/shard_map/ppermute | solution.py:355
  5.6 17.4 %collective-permute-start.11 = (f32[480,128]{1,0:T(8,128)S(1)}, f32[480,128]{1,0:T(8,128)S(1)}, u32[]{:S(2)}, u32[]{:S(2)}) collective-permute-start(f32[480,128]{1,0:T(8,128)S(1)} %slice_bitcast_fusion.prev.nxt.cur.refs_6_), channel_id=1, source_target_pairs={{0,30},{2,4},{4,2},{6,8},{8,6},{10,12},{12,10},{14,16},{16,14},{18... | collective-permute-start | bytes 737288 | tf_op jit(solution)/shard_map/ppermute | solution.py:355
  5.7 20.7 %collective-permute-start.5 = (f32[480,128]{1,0:T(8,128)S(1)}, f32[480,128]{1,0:T(8,128)S(1)}, u32[]{:S(2)}, u32[]{:S(2)}) collective-permute-start(f32[480,128]{1,0:T(8,128)S(1)} %get-tuple-element.20.nxt.cur.field.refs_6_.prev), channel_id=1, source_target_pairs={{0,30},{2,4},{4,2},{6,8},{8,6},{10,12},{12,10},{14,16},{16,14},{18... | collective-permute-start | bytes 737288 | tf_op jit(solution)/shard_map/ppermute | solution.py:355
  7.3 21.0 %collective-permute-start.1 = (f32[480,128]{1,0:T(8,128)S(1)}, f32[480,128]{1,0:T(8,128)}, u32[]{:S(2)}, u32[]{:S(2)}) collective-permute-start(f32[480,128]{1,0:T(8,128)S(1)} %get-tuple-element.22.cur.refs_6_.nxt.prev), channel_id=1, source_target_pairs={{0,30},{2,4},{4,2},{6,8},{8,6},{10,12},{12,10},{14,16},{16,14},{18... | collective-permute-start | bytes 737288 | tf_op jit(solution)/shard_map/ppermute | solution.py:355
  20.2 5.0 %copy-start = (f32[60,1,32,128]{3,2,1,0:T(8,128)S(1)}, f32[60,1,32,128]{3,2,1,0:T(8,128)}, u32[]{:S(2)}) copy-start(f32[60,1,32,128]{3,2,1,0:T(8,128)} %param.9) | copy-start | bytes 2949124
  20.2 12.6 %collective-permute-start.4 = (f32[480,128]{1,0:T(8,128)}, f32[480,128]{1,0:T(8,128)}, u32[]{:S(2)}, u32[]{:S(2)}) collective-permute-start(f32[480,128]{1,0:T(8,128)} %lap.10.refs_7_), channel_id=1, source_target_pairs={{0,1},{1,0},{2,3},{3,2},{4,5},{5,4},{6,7},{7,6},{8,9},{9,8},{10,11... | collective-permute-start | bytes 737288 | tf_op jit(solution)/shard_map/ppermute | solution.py:363
  23.1 2.1 %copy-start.4 = (s32[1,32,128]{2,1,0:T(8,128)S(1)}, s32[1,32,128]{2,1,0:T(8,128)}, u32[]{:S(2)}) copy-start(s32[1,32,128]{2,1,0:T(8,128)} %param.12) | copy-start | bytes 49156
  23.3 11.9 %collective-permute-start.12 = (f32[480,128]{1,0:T(8,128)S(1)}, f32[480,128]{1,0:T(8,128)}, u32[]{:S(2)}, u32[]{:S(2)}) collective-permute-start(f32[480,128]{1,0:T(8,128)S(1)} %lap.13.refs_7_), channel_id=1, source_target_pairs={{0,1},{1,0},{2,3},{3,2},{4,5},{5,4},{6,7},{7,6},{8,9},{9,8},{10,11... | collective-permute-start | bytes 737288 | tf_op jit(solution)/shard_map/ppermute | solution.py:363
  25.9 13.0 %collective-permute-start.7 = (f32[480,128]{1,0:T(8,128)}, f32[480,128]{1,0:T(8,128)}, u32[]{:S(2)}, u32[]{:S(2)}) collective-permute-start(f32[480,128]{1,0:T(8,128)} %blend.1), channel_id=1, source_target_pairs={{0,1},{1,0},{2,3},{3,2},{4,5},{5,4},{6,7},{7,6},{8,9},{9,8},{10,11... | collective-permute-start | bytes 737288 | tf_op jit(solution)/shard_map/ppermute | solution.py:363
  26.6 15.5 %collective-permute-start.6 = (f32[480,128]{1,0:T(8,128)S(1)}, f32[480,128]{1,0:T(8,128)}, u32[]{:S(2)}, u32[]{:S(2)}) collective-permute-start(f32[480,128]{1,0:T(8,128)S(1)} %lap.11.refs_7_), channel_id=1, source_target_pairs={{0,1},{1,0},{2,3},{3,2},{4,5},{5,4},{6,7},{7,6},{8,9},{9,8},{10,11... | collective-permute-start | bytes 737288 | tf_op jit(solution)/shard_map/ppermute | solution.py:363
  28.3 3.0 %copy-start.1 = (f32[7,1,32,128]{3,2,1,0:T(8,128)S(1)}, f32[7,1,32,128]{3,2,1,0:T(8,128)}, u32[]{:S(2)}) copy-start(f32[7,1,32,128]{3,2,1,0:T(8,128)} %param.13) | copy-start | bytes 344068
  29.5 15.4 %collective-permute-start.2 = (f32[480,128]{1,0:T(8,128)S(1)}, f32[480,128]{1,0:T(8,128)S(1)}, u32[]{:S(2)}, u32[]{:S(2)}) collective-permute-start(f32[480,128]{1,0:T(8,128)S(1)} %lap.9.refs_7_), channel_id=1, source_target_pairs={{0,1},{1,0},{2,3},{3,2},{4,5},{5,4},{6,7},{7,6},{8,9},{9,8},{10,11... | collective-permute-start | bytes 737288 | tf_op jit(solution)/shard_map/ppermute | solution.py:363
  34.5 11.8 %collective-permute-start.15 = (f32[480,128]{1,0:T(8,128)S(1)}, f32[480,128]{1,0:T(8,128)S(1)}, u32[]{:S(2)}, u32[]{:S(2)}) collective-permute-start(f32[480,128]{1,0:T(8,128)S(1)} %final.8.prev.cur.nxt.refs_6_), channel_id=1, source_target_pairs={{0,2},{2,0},{4,6},{6,4},{8,10},{10,8},{12,14},{14,12},{16,18},{18,... | collective-permute-start | bytes 737288 | tf_op jit(solution)/shard_map/ppermute | solution.py:349
  35.1 12.8 %collective-permute-start.16 = (f32[480,128]{1,0:T(8,128)S(1)}, f32[480,128]{1,0:T(8,128)S(1)}, u32[]{:S(2)}, u32[]{:S(2)}) collective-permute-start(f32[480,128]{1,0:T(8,128)S(1)} %final.8.prev.cur.nxt.refs_6_), channel_id=1, source_target_pairs={{0,30},{2,4},{4,2},{6,8},{8,6},{10,12},{12,10},{14,16},{16,14},{18... | collective-permute-start | bytes 737288 | tf_op jit(solution)/shard_map/ppermute | solution.py:355
  38.9 11.4 %collective-permute-start.18 = (f32[480,128]{1,0:T(8,128)S(1)}, f32[480,128]{1,0:T(8,128)S(1)}, u32[]{:S(2)}, u32[]{:S(2)}) collective-permute-start(f32[480,128]{1,0:T(8,128)S(1)} %final.10.nxt.prev.cur.refs_6_), channel_id=1, source_target_pairs={{0,2},{2,0},{4,6},{6,4},{8,10},{10,8},{12,14},{14,12},{16,18},{18,... | collective-permute-start | bytes 737288 | tf_op jit(solution)/shard_map/ppermute | solution.py:349
  42.1 8.4 %collective-permute-start.19 = (f32[480,128]{1,0:T(8,128)S(1)}, f32[480,128]{1,0:T(8,128)S(1)}, u32[]{:S(2)}, u32[]{:S(2)}) collective-permute-start(f32[480,128]{1,0:T(8,128)S(1)} %final.10.nxt.prev.cur.refs_6_), channel_id=1, source_target_pairs={{0,30},{2,4},{4,2},{6,8},{8,6},{10,12},{12,10},{14,16},{16,14},{18... | collective-permute-start | bytes 737288 | tf_op jit(solution)/shard_map/ppermute | solution.py:355
  44.9 24.5 %collective-permute-start.13 = (f32[960,128]{1,0:T(8,128)S(1)}, f32[960,128]{1,0:T(8,128)S(1)}, u32[]{:S(2)}, u32[]{:S(2)}) collective-permute-start(f32[960,128]{1,0:T(8,128)S(1)} %final.9.nxt.cur.prev.refs_10_), channel_id=1, source_target_pairs={{0,2},{2,0},{4,6},{6,4},{8,10},{10,8},{12,14},{14,12},{16,18},{18,... | collective-permute-start | bytes 1474568 | tf_op jit(solution)/shard_map/ppermute | solution.py:349
  46.3 23.1 %collective-permute-start.14 = (f32[960,128]{1,0:T(8,128)S(1)}, f32[960,128]{1,0:T(8,128)S(1)}, u32[]{:S(2)}, u32[]{:S(2)}) collective-permute-start(f32[960,128]{1,0:T(8,128)S(1)} %final.9.nxt.cur.prev.refs_10_), channel_id=1, source_target_pairs={{0,30},{2,4},{4,2},{6,8},{8,6},{10,12},{12,10},{14,16},{16,14},{18... | collective-permute-start | bytes 1474568 | tf_op jit(solution)/shard_map/ppermute | solution.py:355
  48.0 3.9 %collective-permute-start.8 = (f32[480,128]{1,0:T(8,128)S(1)}, f32[480,128]{1,0:T(8,128)S(1)}, u32[]{:S(2)}, u32[]{:S(2)}) collective-permute-start(f32[480,128]{1,0:T(8,128)S(1)} %final.7.cur.prev.nxt.refs_6_), channel_id=1, source_target_pairs={{0,2},{2,0},{4,6},{6,4},{8,10},{10,8},{12,14},{14,12},{16,18},{18,... | collective-permute-start | bytes 737288 | tf_op jit(solution)/shard_map/ppermute | solution.py:349
  50.3 16.1 %collective-permute-start.9 = (f32[480,128]{1,0:T(8,128)S(1)}, f32[480,128]{1,0:T(8,128)S(1)}, u32[]{:S(2)}, u32[]{:S(2)}) collective-permute-start(f32[480,128]{1,0:T(8,128)S(1)} %final.7.cur.prev.nxt.refs_6_), channel_id=1, source_target_pairs={{0,30},{2,4},{4,2},{6,8},{8,6},{10,12},{12,10},{14,16},{16,14},{18... | collective-permute-start | bytes 737288 | tf_op jit(solution)/shard_map/ppermute | solution.py:355
  50.5 19.2 %collective-permute-start.17 = (f32[608,128]{1,0:T(8,128)S(1)}, f32[608,128]{1,0:T(8,128)S(1)}, u32[]{:S(2)}, u32[]{:S(2)}) collective-permute-start(f32[608,128]{1,0:T(8,128)S(1)} %lap.15.refs_7_), channel_id=1, source_target_pairs={{0,1},{1,0},{2,3},{3,2},{4,5},{5,4},{6,7},{7,6},{8,9},{9,8},{10,11... | collective-permute-start | bytes 933896 | tf_op jit(solution)/shard_map/ppermute | solution.py:363
  51.9 19.4 %collective-permute-start.20 = (f32[480,128]{1,0:T(8,128)S(1)}, f32[480,128]{1,0:T(8,128)S(1)}, u32[]{:S(2)}, u32[]{:S(2)}) collective-permute-start(f32[480,128]{1,0:T(8,128)S(1)} %lap.17.refs_7_), channel_id=1, source_target_pairs={{0,1},{1,0},{2,3},{3,2},{4,5},{5,4},{6,7},{7,6},{8,9},{9,8},{10,11... | collective-permute-start | bytes 737288 | tf_op jit(solution)/shard_map/ppermute | solution.py:363
  66.6 6.1 %collective-permute-start.10 = (f32[480,128]{1,0:T(8,128)S(1)}, f32[480,128]{1,0:T(8,128)S(1)}, u32[]{:S(2)}, u32[]{:S(2)}) collective-permute-start(f32[480,128]{1,0:T(8,128)S(1)} %lap.12.refs_7_), channel_id=1, source_target_pairs={{0,1},{1,0},{2,3},{3,2},{4,5},{5,4},{6,7},{7,6},{8,9},{9,8},{10,11... | collective-permute-start | bytes 737288 | tf_op jit(solution)/shard_map/ppermute | solution.py:363
  (4 other events, 6.8 us)

commit v2 on v1

--- a/solution.py
+++ b/solution.py
@@ -114,17 +114,6 @@
     couple(n, chunk, blocks, fields, matrices.at[0], lap, rhs, mixed, emit)
 
 
-def blend_kernel(n, chunk, slope, average, metal, field, source, out):
-    nz = field.shape[1]
-    here, _, step = cell_factors(chunk, slope, average, metal)
-    g = group_of(n)
-    for j in range(0, n, g):
-        rows = pl.ds(j * ROWS, g * ROWS)
-        u = field[rows, :].reshape(g, ROWS, nz)
-        v = u + step * (source[pl.ds(j, g)] - here * u)
-        out[rows, :] = v.reshape(g * ROWS, nz)
-
-
 def final_kernel(n, entries, last, double, *refs):
     fields, slope, average, metal, matrices, source = refs[:6]
     refs = refs[6:]
@@ -222,10 +211,6 @@
     return pl.BlockSpec(a.shape, lambda i, d=len(a.shape): (0,) * d)
 
 
-def rows_of(a, chunk):
-    return pl.BlockSpec((a.shape[0], ROWS, a.shape[2]), lambda i: (0, chunk, 0))
-
-
 def estimate(flops, moved):
     return pl.CostEstimate(flops=flops, bytes_accessed=4 * moved, transcendentals=0)
 
@@ -266,22 +251,6 @@
         name="own",
         cost_estimate=estimate(6 * blocks * kl * n * size, 2 * size),
     )(fields, matrices, lap)
-
-
-def blend_call(n, chunk, shared, field, source):
-    nz = field.shape[1]
-    size = n * ROWS * nz
-    operands = [*shared[1:], field, source]
-    return pl.pallas_call(
-        functools.partial(blend_kernel, n, chunk),
-        grid=(1,),
-        out_shape=jax.ShapeDtypeStruct((n * ROWS, nz), F32),
-        in_specs=[*(whole(a) for a in operands[:-1]), rows_of(source, chunk)],
-        out_specs=pl.BlockSpec((n * ROWS, nz), lambda i: (0, 0)),
-        compiler_params=params(),
-        name="blend",
-        cost_estimate=estimate(4 * size, 3 * size),
-    )(*operands)
 
 
 def final_call(n, chunks, last, shared, matrices, source, parts, blended, outs):
@@ -385,7 +354,11 @@
     near_whole = near_swap(u0)
     blended = None
     if double:
-        blended = blend_call(n, tail, shared, field[tail][0], source)
+        _, slope, average, metal = (a[..., tail * ROWS : count * ROWS, :] for a in shared)
+        step = RELAXATION / (slope + 6.0 * average * (1.0 + 3.0 * metal.astype(F32)))
+        u = u0[:, tail * ROWS : count * ROWS]
+        v = u + step * (source[:, tail * ROWS : count * ROWS] - slope * u)
+        blended = v.reshape(n * ROWS, nz)
         (blended,) = to_others(blended)
     outs = ()
     for turn in range(ROUNDS):

time: 75.3 us -> 74.7 us (level)
  waiting for transfers between devices: 29 us -> 34.9 us
  Pallas kernels: 20.5 us -> 15.9 us
  starting transfers between devices: 22.4 us -> 19.5 us
  other arithmetic: 0 us -> 2.1 us
  local copies, waits for them, and re-layouts: 2.23 us -> 1.01 us
    ppermute x8, waiting for transfers between devices: 1.52 us -> 5.24 us  [to_others(): got.append(lax.ppermute(x, 'modes', ring))]
    ppermute x5, starting transfers between devices: 6.52 us -> 3.69 us  [near_swap(): return lax.ppermute(x, 'space', [(i, i ^ 1) for i in range(count)])]
    ppermute x8, waiting for transfers between devices: 27.4 us -> 29.7 us  [far_swap(): return lax.ppermute(x, 'space', pairs)]
    pallas_call x7, Pallas kernels: 11 us -> 8.86 us  [final_call(): pl.pallas_call(functools.partial(final_kernel, n, tuple(entries), last, d...]
    reshape x0 -> x1, other arithmetic: none -> 2.09 us  [rounds(): blended = v.reshape(n * ROWS, nz)]
    reshape x2 -> x1, local copies, waits for them, and re-layouts: 2.2 us -> 0.98 us  [rounds(): cut = lambda c: u0[:, c * ROWS:(c + 1) * ROWS].reshape(n * ROWS, nz)]
    pallas_call x7, Pallas kernels: 4.76 us -> 3.81 us  [own_call(): pl.pallas_call(functools.partial(own_kernel, n, chunk, blocks), out_shape...]
    ppermute x8, starting transfers between devices: 6.18 us -> 7.06 us  [far_swap(): return lax.ppermute(x, 'space', pairs)]
  transfers between devices with their start and end apart: 21 -> 21, of which waited for: 5 -> 8; matrix products, arithmetic and copies ran while one was open for 2% -> 3% of each run, Pallas kernels for 24% -> 18%
where the time goes in v2:
time: 74.7 us; the launch traced here: 74.4 us
  waiting for transfers between devices  34.9 us (47%)
  starting transfers between devices  19.5 us (26%)
  Pallas kernels  15.9 us (21%)
  other arithmetic  2.1 us (3%)
  local copies, waits for them, and re-layouts  1.01 us (1%)
  between operations  0.95 us (1%)
    ppermute x8, waiting for transfers between devices, far_swap(): return lax.ppermute(x, 'space', pairs)  29.7 us
    pallas_call x7, Pallas kernels, final_call(): pl.pallas_call(functools.partial(final_kernel, n, tuple(entries), last, d...  8.86 us
    ppermute x8, starting transfers between devices, to_others(): got.append(lax.ppermute(x, 'modes', ring))  8.79 us
    ppermute x8, starting transfers between devices, far_swap(): return lax.ppermute(x, 'space', pairs)  7.06 us
    ppermute x8, waiting for transfers between devices, to_others(): got.append(lax.ppermute(x, 'modes', ring))  5.24 us
    pallas_call x7, Pallas kernels, own_call(): pl.pallas_call(functools.partial(own_kernel, n, chunk, blocks), out_shape...  3.81 us
    ppermute x5, starting transfers between devices, near_swap(): return lax.ppermute(x, 'space', [(i, i ^ 1) for i in range(count)])  3.69 us
    pallas_call x9, Pallas kernels, lap_call(): pl.pallas_call(functools.partial(lap_kernel, n, chunk, slots, edge, compa...  2.73 us
  transfers between devices with their start and end apart: 21, of which 8 were waited for; matrix products, arithmetic and copies ran while one was open for 3% of the time, Pallas kernels for 18%

profile of v2, /device:TPU:1, one launch (start us, length us, event | category | flops | bytes accessed | tf_op | source)
XLA Modules:
  0.0 74.4 jit_solution(12446958091800677970)
XLA Ops:
  0.7 1.0 %slice_bitcast_fusion.prev.nxt.cur.refs_6_ = f32[480,128]{1,0:T(8,128)S(1)} fusion(f32[60,32,128]{2,1,0:T(8,128)} %bitcast.74), kind=kLoop, calls=%fused_computation.4 | loop fusion | bytes 491520 | tf_op jit(solution)/shard_map/reshape | solution.py:347
  1.8 2.1 %fusion.2 = (f32[480,128]{1,0:T(8,128)}, f32[480,128]{1,0:T(8,128)S(1)}, f32[480,128]{1,0:T(8,128)S(1)}, f32[480,128]{1,0:T(8,128)S(1)}) fusion(f32[60,32,128]{2,1,0:T(8,128)} %bitcast.28, f32[60,32,128]{2,1,0:T(8,128)} %bitcast.76, f32[8,128]{1,0:T(8,128)S(1)} %get-tuple-element.25, f32[8,128]{1,0:T(8,128)S(1)} %get-tuple-element.24), kind=kLoop, calls=%fused_computation.3 | loop fusion | flops 245760 | bytes 1974272 | tf_op jit(solution)/shard_map/reshape | solution.py:361
  3.9 2.6 %collective-permute-start.3 = (f32[480,128]{1,0:T(8,128)S(1)}, f32[480,128]{1,0:T(8,128)S(1)}, u32[]{:S(2)}, u32[]{:S(2)}) collective-permute-start(f32[480,128]{1,0:T(8,128)S(1)} %get-tuple-element.22.prev.cur.refs_6_.nxt), channel_id=1, source_target_pairs={{0,30},{2,4},{4,2},{6,8},{8,6},{10,12},{12,10},{14,16},{16,14},{18... | collective-permute-start | bytes 737288 | tf_op jit(solution)/shard_map/ppermute | solution.py:324
  6.5 1.7 %collective-permute-start.5 = (f32[480,128]{1,0:T(8,128)S(1)}, f32[480,128]{1,0:T(8,128)S(1)}, u32[]{:S(2)}, u32[]{:S(2)}) collective-permute-start(f32[480,128]{1,0:T(8,128)S(1)} %get-tuple-element.21.nxt.cur.refs_6_.prev), channel_id=1, source_target_pairs={{0,30},{2,4},{4,2},{6,8},{8,6},{10,12},{12,10},{14,16},{16,14},{18... | collective-permute-start | bytes 737288 | tf_op jit(solution)/shard_map/ppermute | solution.py:324
  8.3 11.9 %collective-permute-done.3.far = f32[480,128]{1,0:T(8,128)S(1)} collective-permute-done((f32[480,128]{1,0:T(8,128)S(1)}, f32[480,128]{1,0:T(8,128)S(1)}, u32[]{:S(2)}, u32[]{:S(2)}) %collective-permute-start.3) | collective-permute-done | bytes 245792 | tf_op jit(solution)/shard_map/ppermute | solution.py:324
  20.4 1.3 %collective-permute-start.4 = (f32[480,128]{1,0:T(8,128)S(1)}, f32[480,128]{1,0:T(8,128)}, u32[]{:S(2)}, u32[]{:S(2)}) collective-permute-start(f32[480,128]{1,0:T(8,128)S(1)} %lap.10.refs_7_), channel_id=1, source_target_pairs={{0,1},{1,0},{2,3},{3,2},{4,5},{5,4},{6,7},{7,6},{8,9},{9,8},{10,11... | collective-permute-start | bytes 737288 | tf_op jit(solution)/shard_map/ppermute | solution.py:332
  21.6 2.2 %collective-permute-done.11.far = f32[480,128]{1,0:T(8,128)S(1)} collective-permute-done((f32[480,128]{1,0:T(8,128)S(1)}, f32[480,128]{1,0:T(8,128)S(1)}, u32[]{:S(2)}, u32[]{:S(2)}) %collective-permute-start.11) | collective-permute-done | bytes 245792 | tf_op jit(solution)/shard_map/ppermute | solution.py:324
  24.0 1.9 %collective-permute-start.12 = (f32[480,128]{1,0:T(8,128)S(1)}, f32[480,128]{1,0:T(8,128)S(1)}, u32[]{:S(2)}, u32[]{:S(2)}) collective-permute-start(f32[480,128]{1,0:T(8,128)S(1)} %lap.13.refs_7_), channel_id=1, source_target_pairs={{0,1},{1,0},{2,3},{3,2},{4,5},{5,4},{6,7},{7,6},{8,9},{9,8},{10,11... | collective-permute-start | bytes 737288 | tf_op jit(solution)/shard_map/ppermute | solution.py:332
  26.7 1.9 %collective-permute-start.6 = (f32[480,128]{1,0:T(8,128)S(1)}, f32[480,128]{1,0:T(8,128)S(1)}, u32[]{:S(2)}, u32[]{:S(2)}) collective-permute-start(f32[480,128]{1,0:T(8,128)S(1)} %lap.11.refs_7_), channel_id=1, source_target_pairs={{0,1},{1,0},{2,3},{3,2},{4,5},{5,4},{6,7},{7,6},{8,9},{9,8},{10,11... | collective-permute-start | bytes 737288 | tf_op jit(solution)/shard_map/ppermute | solution.py:332
  29.1 1.2 %lap.9.refs_7_ = f32[480,128]{1,0:T(8,128)S(1)} custom-call(f32[480,128]{1,0:T(8,128)S(1)} %get-tuple-element.22.prev.cur.refs_6_.nxt, f32[480,128]{1,0:T(8,128)S(1)} %get-tuple-element.23.cur.refs_6_.nxt.prev, f32[480,128]{1,0:T(8,128)S(1)} %get-tuple-element.21.nxt.cur.refs_6_.prev, f32[60,32,128]{2,1,0:T(8,128)S(1)} %collective-permute-done.near, ...), custom_call_target="tpu_custom_call" | custom-call | flops 737280 | bytes 1474560 | tf_op jit(solution)/shard_map/lap/pallas_call | solution.py:230
  30.3 1.8 %collective-permute-start.2 = (f32[480,128]{1,0:T(8,128)S(1)}, f32[480,128]{1,0:T(8,128)S(1)}, u32[]{:S(2)}, u32[]{:S(2)}) collective-permute-start(f32[480,128]{1,0:T(8,128)S(1)} %lap.9.refs_7_), channel_id=1, source_target_pairs={{0,1},{1,0},{2,3},{3,2},{4,5},{5,4},{6,7},{7,6},{8,9},{9,8},{10,11... | collective-permute-start | bytes 737288 | tf_op jit(solution)/shard_map/ppermute | solution.py:332
  32.6 1.6 %final.8.prev.cur.nxt.refs_6_ = f32[480,128]{1,0:T(8,128)S(1)} custom-call(f32[7,32,128]{2,1,0:T(8,128)S(1)} %bitcast.37, f32[32,128]{1,0:T(8,128)S(1)} %bitcast.50, f32[32,128]{1,0:T(8,128)S(1)} %bitcast.57, s32[32,128]{1,0:T(8,128)S(1)} %bitcast.64, bf16[2,896,192]{2,1,0:T(8,128)(2,1)S(1)} %coupling.1.matrices.refs_4_, f32[60,32,128]{2,1,0:T(8,128)S(1)} %bitcast.29, ...), custom_call_target="tpu_custom_call" | custom-call | flops 154828800 | bytes 1474560 | tf_op jit(solution)/shard_map/final/pallas_call | solution.py:282
  34.8 1.3 %collective-permute-start.16 = (f32[480,128]{1,0:T(8,128)S(1)}, f32[480,128]{1,0:T(8,128)S(1)}, u32[]{:S(2)}, u32[]{:S(2)}) collective-permute-start(f32[480,128]{1,0:T(8,128)S(1)} %final.8.prev.cur.nxt.refs_6_), channel_id=1, source_target_pairs={{0,30},{2,4},{4,2},{6,8},{8,6},{10,12},{12,10},{14,16},{16,14},{18... | collective-permute-start | bytes 737288 | tf_op jit(solution)/shard_map/ppermute | solution.py:324
  36.8 2.1 %collective-permute-done.7.refs_10_ = f32[480,128]{1,0:T(8,128)S(1)} collective-permute-done((f32[480,128]{1,0:T(8,128)}, f32[480,128]{1,0:T(8,128)S(1)}, u32[]{:S(2)}, u32[]{:S(2)}) %collective-permute-start.7) | collective-permute-done | bytes 245792 | tf_op jit(solution)/shard_map/ppermute | solution.py:332
  38.9 1.5 %collective-permute-start.18 = (f32[480,128]{1,0:T(8,128)S(1)}, f32[480,128]{1,0:T(8,128)S(1)}, u32[]{:S(2)}, u32[]{:S(2)}) collective-permute-start(f32[480,128]{1,0:T(8,128)S(1)} %final.10.nxt.prev.cur.refs_6_), channel_id=1, source_target_pairs={{0,2},{2,0},{4,6},{6,4},{8,10},{10,8},{12,14},{14,12},{16,18},{18,... | collective-permute-start | bytes 737288 | tf_op jit(solution)/shard_map/ppermute | solution.py:318
  40.4 2.5 %collective-permute-done.6.refs_9_ = f32[480,128]{1,0:T(8,128)S(1)} collective-permute-done((f32[480,128]{1,0:T(8,128)S(1)}, f32[480,128]{1,0:T(8,128)S(1)}, u32[]{:S(2)}, u32[]{:S(2)}) %collective-permute-start.6) | collective-permute-done | bytes 245792 | tf_op jit(solution)/shard_map/ppermute | solution.py:332
  43.7 1.0 %final.9.nxt.cur.prev.refs_10_ = f32[960,128]{1,0:T(8,128)S(1)} custom-call(f32[7,32,128]{2,1,0:T(8,128)S(1)} %bitcast.41, f32[32,128]{1,0:T(8,128)S(1)} %bitcast.52, f32[32,128]{1,0:T(8,128)S(1)} %bitcast.59, s32[32,128]{1,0:T(8,128)S(1)} %bitcast.66, bf16[2,896,192]{2,1,0:T(8,128)(2,1)S(1)} %coupling.1.matrices.refs_4_, f32[60,32,128]{2,1,0:T(8,128)S(1)} %bitcast.31, ...), custom_call_target="tpu_custom_call" | custom-call | flops 309657600 | bytes 1474560 | tf_op jit(solution)/shard_map/final/pallas_call | solution.py:282
  45.2 1.3 %collective-permute-start.14 = (f32[960,128]{1,0:T(8,128)S(1)}, f32[960,128]{1,0:T(8,128)S(1)}, u32[]{:S(2)}, u32[]{:S(2)}) collective-permute-start(f32[960,128]{1,0:T(8,128)S(1)} %final.9.nxt.cur.prev.refs_10_), channel_id=1, source_target_pairs={{0,30},{2,4},{4,2},{6,8},{8,6},{10,12},{12,10},{14,16},{16,14},{18... | collective-permute-start | bytes 1474568 | tf_op jit(solution)/shard_map/ppermute | solution.py:324
  47.7 2.1 %collective-permute-start.8 = (f32[480,128]{1,0:T(8,128)S(1)}, f32[480,128]{1,0:T(8,128)S(1)}, u32[]{:S(2)}, u32[]{:S(2)}) collective-permute-start(f32[480,128]{1,0:T(8,128)S(1)} %final.7.cur.prev.nxt.refs_6_), channel_id=1, source_target_pairs={{0,2},{2,0},{4,6},{6,4},{8,10},{10,8},{12,14},{14,12},{16,18},{18,... | collective-permute-start | bytes 737288 | tf_op jit(solution)/shard_map/ppermute | solution.py:318
  51.5 1.0 %collective-permute-start.20 = (f32[480,128]{1,0:T(8,128)S(1)}, f32[480,128]{1,0:T(8,128)S(1)}, u32[]{:S(2)}, u32[]{:S(2)}) collective-permute-start(f32[480,128]{1,0:T(8,128)S(1)} %lap.17.refs_7_), channel_id=1, source_target_pairs={{0,1},{1,0},{2,3},{3,2},{4,5},{5,4},{6,7},{7,6},{8,9},{9,8},{10,11... | collective-permute-start | bytes 737288 | tf_op jit(solution)/shard_map/ppermute | solution.py:332
  52.5 14.3 %collective-permute-done.9.far = f32[480,128]{1,0:T(8,128)S(1)} collective-permute-done((f32[480,128]{1,0:T(8,128)S(1)}, f32[480,128]{1,0:T(8,128)S(1)}, u32[]{:S(2)}, u32[]{:S(2)}) %collective-permute-start.9) | collective-permute-done | bytes 245792 | tf_op jit(solution)/shard_map/ppermute | solution.py:324
  69.4 1.4 %final.11 = (f32[60,32,128]{2,1,0:T(8,128)}, f32[60,32,128]{2,1,0:T(8,128)}) custom-call(f32[7,32,128]{2,1,0:T(8,128)S(1)} %bitcast.47, f32[32,128]{1,0:T(8,128)S(1)} %bitcast.54, f32[32,128]{1,0:T(8,128)S(1)} %bitcast.61, s32[32,128]{1,0:T(8,128)S(1)} %bitcast.68, bf16[2,896,192]{2,1,0:T(8,128)(2,1)S(1)} %coupling.1.matrices.refs_4_, ...), custom_call_target="tpu_custom_call" | custom-call | flops 154828800 | bytes 1474560 | tf_op jit(solution)/shard_map/final/pallas_call | solution.py:282
  70.8 1.4 %final.12 = (f32[60,32,128]{2,1,0:T(8,128)}, f32[60,32,128]{2,1,0:T(8,128)}) custom-call(f32[7,32,128]{2,1,0:T(8,128)S(1)} %bitcast.48, f32[32,128]{1,0:T(8,128)S(1)} %bitcast.55, f32[32,128]{1,0:T(8,128)S(1)} %bitcast.62, s32[32,128]{1,0:T(8,128)S(1)} %bitcast.69, ...), custom_call_target="tpu_custom_call", output_to_operand_aliasing={{0}: (10, {}), {1}: (11, {})} | custom-call | flops 154828800 | bytes 1474560 | tf_op jit(solution)/shard_map/final/pallas_call | solution.py:282
  72.2 2.2 %final.13 = (f32[60,32,128]{2,1,0:T(8,128)}, f32[60,32,128]{2,1,0:T(8,128)}) custom-call(f32[7,32,128]{2,1,0:T(8,128)S(1)} %bitcast.49, f32[32,128]{1,0:T(8,128)S(1)} %bitcast.56, f32[32,128]{1,0:T(8,128)S(1)} %bitcast.63, s32[32,128]{1,0:T(8,128)S(1)} %bitcast.70, ...), custom_call_target="tpu_custom_call", output_to_operand_aliasing={{0}: (13, {}), {1}: (14, {})} | custom-call | flops 309657600 | bytes 2949120 | tf_op jit(solution)/shard_map/final/pallas_call | solution.py:282
  (59 shorter events, 10.2 us)
Async XLA Ops:
  1.6 18.5 %collective-permute-start = (f32[60,32,128]{2,1,0:T(8,128)}, f32[60,32,128]{2,1,0:T(8,128)S(1)}, u32[]{:S(2)}, u32[]{:S(2)}) collective-permute-start(f32[60,32,128]{2,1,0:T(8,128)} %bitcast.75), channel_id=1, source_target_pairs={{0,2},{2,0},{4,6},{6,4},{8,10},{10,8},{12,14},{14,12},{16,18},{18,... | collective-permute-start | bytes 2949128 | tf_op jit(solution)/shard_map/ppermute | solution.py:318
  3.9 16.3 %collective-permute-start.3 = (f32[480,128]{1,0:T(8,128)S(1)}, f32[480,128]{1,0:T(8,128)S(1)}, u32[]{:S(2)}, u32[]{:S(2)}) collective-permute-start(f32[480,128]{1,0:T(8,128)S(1)} %get-tuple-element.22.prev.cur.refs_6_.nxt), channel_id=1, source_target_pairs={{0,30},{2,4},{4,2},{6,8},{8,6},{10,12},{12,10},{14,16},{16,14},{18... | collective-permute-start | bytes 737288 | tf_op jit(solution)/shard_map/ppermute | solution.py:324
  6.5 17.3 %collective-permute-start.11 = (f32[480,128]{1,0:T(8,128)S(1)}, f32[480,128]{1,0:T(8,128)S(1)}, u32[]{:S(2)}, u32[]{:S(2)}) collective-permute-start(f32[480,128]{1,0:T(8,128)S(1)} %slice_bitcast_fusion.prev.nxt.cur.refs_6_), channel_id=1, source_target_pairs={{0,30},{2,4},{4,2},{6,8},{8,6},{10,12},{12,10},{14,16},{16,14},{18... | collective-permute-start | bytes 737288 | tf_op jit(solution)/shard_map/ppermute | solution.py:324
  6.5 20.0 %collective-permute-start.5 = (f32[480,128]{1,0:T(8,128)S(1)}, f32[480,128]{1,0:T(8,128)S(1)}, u32[]{:S(2)}, u32[]{:S(2)}) collective-permute-start(f32[480,128]{1,0:T(8,128)S(1)} %get-tuple-element.21.nxt.cur.refs_6_.prev), channel_id=1, source_target_pairs={{0,30},{2,4},{4,2},{6,8},{8,6},{10,12},{12,10},{14,16},{16,14},{18... | collective-permute-start | bytes 737288 | tf_op jit(solution)/shard_map/ppermute | solution.py:324
  8.2 20.9 %collective-permute-start.1 = (f32[480,128]{1,0:T(8,128)S(1)}, f32[480,128]{1,0:T(8,128)}, u32[]{:S(2)}, u32[]{:S(2)}) collective-permute-start(f32[480,128]{1,0:T(8,128)S(1)} %get-tuple-element.23.cur.refs_6_.nxt.prev), channel_id=1, source_target_pairs={{0,30},{2,4},{4,2},{6,8},{8,6},{10,12},{12,10},{14,16},{16,14},{18... | collective-permute-start | bytes 737288 | tf_op jit(solution)/shard_map/ppermute | solution.py:324
  20.4 12.3 %collective-permute-start.4 = (f32[480,128]{1,0:T(8,128)S(1)}, f32[480,128]{1,0:T(8,128)}, u32[]{:S(2)}, u32[]{:S(2)}) collective-permute-start(f32[480,128]{1,0:T(8,128)S(1)} %lap.10.refs_7_), channel_id=1, source_target_pairs={{0,1},{1,0},{2,3},{3,2},{4,5},{5,4},{6,7},{7,6},{8,9},{9,8},{10,11... | collective-permute-start | bytes 737288 | tf_op jit(solution)/shard_map/ppermute | solution.py:332
  24.0 10.8 %collective-permute-start.12 = (f32[480,128]{1,0:T(8,128)S(1)}, f32[480,128]{1,0:T(8,128)S(1)}, u32[]{:S(2)}, u32[]{:S(2)}) collective-permute-start(f32[480,128]{1,0:T(8,128)S(1)} %lap.13.refs_7_), channel_id=1, source_target_pairs={{0,1},{1,0},{2,3},{3,2},{4,5},{5,4},{6,7},{7,6},{8,9},{9,8},{10,11... | collective-permute-start | bytes 737288 | tf_op jit(solution)/shard_map/ppermute | solution.py:332
  25.9 13.1 %collective-permute-start.7 = (f32[480,128]{1,0:T(8,128)}, f32[480,128]{1,0:T(8,128)S(1)}, u32[]{:S(2)}, u32[]{:S(2)}) collective-permute-start(f32[480,128]{1,0:T(8,128)} %get-tuple-element.20), channel_id=1, source_target_pairs={{0,1},{1,0},{2,3},{3,2},{4,5},{5,4},{6,7},{7,6},{8,9},{9,8},{10,11... | collective-permute-start | bytes 737288 | tf_op jit(solution)/shard_map/ppermute | solution.py:332
  26.4 2.1 %copy-start.6 = (f32[7,72]{1,0:T(8,128)S(1)}, f32[7,72]{1,0:T(8,128)}, u32[]{:S(2)}) copy-start(f32[7,72]{1,0:T(8,128)} %entries.1) | copy-start | bytes 6052
  26.7 16.2 %collective-permute-start.6 = (f32[480,128]{1,0:T(8,128)S(1)}, f32[480,128]{1,0:T(8,128)S(1)}, u32[]{:S(2)}, u32[]{:S(2)}) collective-permute-start(f32[480,128]{1,0:T(8,128)S(1)} %lap.11.refs_7_), channel_id=1, source_target_pairs={{0,1},{1,0},{2,3},{3,2},{4,5},{5,4},{6,7},{7,6},{8,9},{9,8},{10,11... | collective-permute-start | bytes 737288 | tf_op jit(solution)/shard_map/ppermute | solution.py:332
  29.0 3.0 %copy-start.1 = (f32[7,1,32,128]{3,2,1,0:T(8,128)S(1)}, f32[7,1,32,128]{3,2,1,0:T(8,128)}, u32[]{:S(2)}) copy-start(f32[7,1,32,128]{3,2,1,0:T(8,128)} %param.13) | copy-start | bytes 344068
  30.3 2.4 %copy-start = (f32[60,1,32,128]{3,2,1,0:T(8,128)S(1)}, f32[60,1,32,128]{3,2,1,0:T(8,128)}, u32[]{:S(2)}) copy-start(f32[60,1,32,128]{3,2,1,0:T(8,128)} %param.9) | copy-start | bytes 2949124
  30.3 15.0 %collective-permute-start.2 = (f32[480,128]{1,0:T(8,128)S(1)}, f32[480,128]{1,0:T(8,128)S(1)}, u32[]{:S(2)}, u32[]{:S(2)}) collective-permute-start(f32[480,128]{1,0:T(8,128)S(1)} %lap.9.refs_7_), channel_id=1, source_target_pairs={{0,1},{1,0},{2,3},{3,2},{4,5},{5,4},{6,7},{7,6},{8,9},{9,8},{10,11... | collective-permute-start | bytes 737288 | tf_op jit(solution)/shard_map/ppermute | solution.py:332
  34.2 11.0 %collective-permute-start.15 = (f32[480,128]{1,0:T(8,128)S(1)}, f32[480,128]{1,0:T(8,128)S(1)}, u32[]{:S(2)}, u32[]{:S(2)}) collective-permute-start(f32[480,128]{1,0:T(8,128)S(1)} %final.8.prev.cur.nxt.refs_6_), channel_id=1, source_target_pairs={{0,2},{2,0},{4,6},{6,4},{8,10},{10,8},{12,14},{14,12},{16,18},{18,... | collective-permute-start | bytes 737288 | tf_op jit(solution)/shard_map/ppermute | solution.py:318
  34.8 12.9 %collective-permute-start.16 = (f32[480,128]{1,0:T(8,128)S(1)}, f32[480,128]{1,0:T(8,128)S(1)}, u32[]{:S(2)}, u32[]{:S(2)}) collective-permute-start(f32[480,128]{1,0:T(8,128)S(1)} %final.8.prev.cur.nxt.refs_6_), channel_id=1, source_target_pairs={{0,30},{2,4},{4,2},{6,8},{8,6},{10,12},{12,10},{14,16},{16,14},{18... | collective-permute-start | bytes 737288 | tf_op jit(solution)/shard_map/ppermute | solution.py:324
  38.9 10.9 %collective-permute-start.18 = (f32[480,128]{1,0:T(8,128)S(1)}, f32[480,128]{1,0:T(8,128)S(1)}, u32[]{:S(2)}, u32[]{:S(2)}) collective-permute-start(f32[480,128]{1,0:T(8,128)S(1)} %final.10.nxt.prev.cur.refs_6_), channel_id=1, source_target_pairs={{0,2},{2,0},{4,6},{6,4},{8,10},{10,8},{12,14},{14,12},{16,18},{18,... | collective-permute-start | bytes 737288 | tf_op jit(solution)/shard_map/ppermute | solution.py:318
  42.9 7.8 %collective-permute-start.19 = (f32[480,128]{1,0:T(8,128)S(1)}, f32[480,128]{1,0:T(8,128)S(1)}, u32[]{:S(2)}, u32[]{:S(2)}) collective-permute-start(f32[480,128]{1,0:T(8,128)S(1)} %final.10.nxt.prev.cur.refs_6_), channel_id=1, source_target_pairs={{0,30},{2,4},{4,2},{6,8},{8,6},{10,12},{12,10},{14,16},{16,14},{18... | collective-permute-start | bytes 737288 | tf_op jit(solution)/shard_map/ppermute | solution.py:324
  45.2 23.7 %collective-permute-start.13 = (f32[960,128]{1,0:T(8,128)S(1)}, f32[960,128]{1,0:T(8,128)S(1)}, u32[]{:S(2)}, u32[]{:S(2)}) collective-permute-start(f32[960,128]{1,0:T(8,128)S(1)} %final.9.nxt.cur.prev.refs_10_), channel_id=1, source_target_pairs={{0,2},{2,0},{4,6},{6,4},{8,10},{10,8},{12,14},{14,12},{16,18},{18,... | collective-permute-start | bytes 1474568 | tf_op jit(solution)/shard_map/ppermute | solution.py:318
  45.2 23.7 %collective-permute-start.14 = (f32[960,128]{1,0:T(8,128)S(1)}, f32[960,128]{1,0:T(8,128)S(1)}, u32[]{:S(2)}, u32[]{:S(2)}) collective-permute-start(f32[960,128]{1,0:T(8,128)S(1)} %final.9.nxt.cur.prev.refs_10_), channel_id=1, source_target_pairs={{0,30},{2,4},{4,2},{6,8},{8,6},{10,12},{12,10},{14,16},{16,14},{18... | collective-permute-start | bytes 1474568 | tf_op jit(solution)/shard_map/ppermute | solution.py:324
  47.7 3.8 %collective-permute-start.8 = (f32[480,128]{1,0:T(8,128)S(1)}, f32[480,128]{1,0:T(8,128)S(1)}, u32[]{:S(2)}, u32[]{:S(2)}) collective-permute-start(f32[480,128]{1,0:T(8,128)S(1)} %final.7.cur.prev.nxt.refs_6_), channel_id=1, source_target_pairs={{0,2},{2,0},{4,6},{6,4},{8,10},{10,8},{12,14},{14,12},{16,18},{18,... | collective-permute-start | bytes 737288 | tf_op jit(solution)/shard_map/ppermute | solution.py:318
  49.8 17.0 %collective-permute-start.9 = (f32[480,128]{1,0:T(8,128)S(1)}, f32[480,128]{1,0:T(8,128)S(1)}, u32[]{:S(2)}, u32[]{:S(2)}) collective-permute-start(f32[480,128]{1,0:T(8,128)S(1)} %final.7.cur.prev.nxt.refs_6_), channel_id=1, source_target_pairs={{0,30},{2,4},{4,2},{6,8},{8,6},{10,12},{12,10},{14,16},{16,14},{18... | collective-permute-start | bytes 737288 | tf_op jit(solution)/shard_map/ppermute | solution.py:324
  50.7 18.4 %collective-permute-start.17 = (f32[608,128]{1,0:T(8,128)S(1)}, f32[608,128]{1,0:T(8,128)S(1)}, u32[]{:S(2)}, u32[]{:S(2)}) collective-permute-start(f32[608,128]{1,0:T(8,128)S(1)} %lap.15.refs_7_), channel_id=1, source_target_pairs={{0,1},{1,0},{2,3},{3,2},{4,5},{5,4},{6,7},{7,6},{8,9},{9,8},{10,11... | collective-permute-start | bytes 933896 | tf_op jit(solution)/shard_map/ppermute | solution.py:332
  51.5 19.3 %collective-permute-start.20 = (f32[480,128]{1,0:T(8,128)S(1)}, f32[480,128]{1,0:T(8,128)S(1)}, u32[]{:S(2)}, u32[]{:S(2)}) collective-permute-start(f32[480,128]{1,0:T(8,128)S(1)} %lap.17.refs_7_), channel_id=1, source_target_pairs={{0,1},{1,0},{2,3},{3,2},{4,5},{5,4},{6,7},{7,6},{8,9},{9,8},{10,11... | collective-permute-start | bytes 737288 | tf_op jit(solution)/shard_map/ppermute | solution.py:332
  67.0 5.2 %collective-permute-start.10 = (f32[480,128]{1,0:T(8,128)S(1)}, f32[480,128]{1,0:T(8,128)S(1)}, u32[]{:S(2)}, u32[]{:S(2)}) collective-permute-start(f32[480,128]{1,0:T(8,128)S(1)} %lap.12.refs_7_), channel_id=1, source_target_pairs={{0,1},{1,0},{2,3},{3,2},{4,5},{5,4},{6,7},{7,6},{8,9},{9,8},{10,11... | collective-permute-start | bytes 737288 | tf_op jit(solution)/shard_map/ppermute | solution.py:332
  (4 other events, 5.2 us)

commit v3 on v2

--- a/solution.py
+++ b/solution.py
@@ -11,6 +11,8 @@
 ROUNDS = 2
 RELAXATION = 0.8
 ROWS = 8
+TOGETHER = 8
+SLOTS = min(2, ROWS // TOGETHER)
 F32, BF16 = jnp.float32, jnp.bfloat16
 
 
@@ -76,10 +78,10 @@
     kl = fields.shape[0]
     wide, tall = ceil_to(n, 16), ceil_to(n, 8)
     used = pl.ds(0, blocks * kl * tall)
-    for pair in range(ROWS // 2):
-        slot = pair % 2
-        for half in range(2):
-            v = lap[pl.ds(2 * pair + half, n, stride=ROWS), :]
+    for part in range(ROWS // TOGETHER):
+        slot = part % SLOTS
+        for half in range(TOGETHER):
+            v = lap[pl.ds(TOGETHER * part + half, n, stride=ROWS), :]
             hi = v.astype(BF16)
             lo = (v - hi.astype(F32)).astype(BF16)
             cols = pl.ds(half * nz, nz)
@@ -87,8 +89,8 @@
             rhs[slot, pl.ds(wide, n), cols] = lo
             rhs[slot, pl.ds(2 * wide, n), cols] = hi
         mixed[slot] = jnp.dot(matrix[used, :], rhs[slot], preferred_element_type=F32)
-        for half in range(2):
-            y = 2 * pair + half
+        for half in range(TOGETHER):
+            y = TOGETHER * part + half
             cols = pl.ds(half * nz, nz)
             for b in range(blocks):
                 total = None
@@ -218,8 +220,8 @@
 def scratch(n, blocks, kl, nz):
     wide, tall = ceil_to(n, 16), ceil_to(n, 8)
     return [
-        pltpu.VMEM((2, 3 * wide, 2 * nz), BF16),
-        pltpu.VMEM((2, blocks * kl * tall, 2 * nz), F32),
+        pltpu.VMEM((SLOTS, 3 * wide, TOGETHER * nz), BF16),
+        pltpu.VMEM((SLOTS, blocks * kl * tall, TOGETHER * nz), F32),
     ]
 
 

time: 74.7 us -> 74.6 us (level)
  transfers between devices with their start and end apart: 21 -> 21, of which waited for: 8 -> 9; matrix products, arithmetic and copies ran while one was open for 3% -> 3% of each run, Pallas kernels for 18% -> 18%
where the time goes in v3:
time: 74.6 us; the launch traced here: 74.3 us
  waiting for transfers between devices  35.2 us (47%)
  starting transfers between devices  19.4 us (26%)
  Pallas kernels  15.6 us (21%)
  other arithmetic  2.1 us (3%)
  local copies, waits for them, and re-layouts  1.01 us (1%)
  between operations  0.95 us (1%)
    ppermute x8, waiting for transfers between devices, far_swap(): return lax.ppermute(x, 'space', pairs)  29.6 us
    ppermute x8, starting transfers between devices, to_others(): got.append(lax.ppermute(x, 'modes', ring))  8.8 us
    pallas_call x7, Pallas kernels, final_call(): pl.pallas_call(functools.partial(final_kernel, n, tuple(entries), last, d...  8.62 us
    ppermute x8, starting transfers between devices, far_swap(): return lax.ppermute(x, 'space', pairs)  6.99 us
    ppermute x8, waiting for transfers between devices, to_others(): got.append(lax.ppermute(x, 'modes', ring))  5.62 us
    pallas_call x7, Pallas kernels, own_call(): pl.pallas_call(functools.partial(own_kernel, n, chunk, blocks), out_shape...  3.7 us
    ppermute x5, starting transfers between devices, near_swap(): return lax.ppermute(x, 'space', [(i, i ^ 1) for i in range(count)])  3.64 us
    pallas_call x9, Pallas kernels, lap_call(): pl.pallas_call(functools.partial(lap_kernel, n, chunk, slots, edge, compa...  2.73 us
  transfers between devices with their start and end apart: 21, of which 9 were waited for; matrix products, arithmetic and copies ran while one was open for 3% of the time, Pallas kernels for 18%

profile of v3, /device:TPU:1, one launch (start us, length us, event | category | flops | bytes accessed | tf_op | source)
XLA Modules:
  0.0 74.3 jit_solution(4198858985531583620)
XLA Ops:
  0.7 1.0 %slice_bitcast_fusion.prev.nxt.cur.refs_6_ = f32[480,128]{1,0:T(8,128)S(1)} fusion(f32[60,32,128]{2,1,0:T(8,128)} %bitcast.74), kind=kLoop, calls=%fused_computation.4 | loop fusion | bytes 491520 | tf_op jit(solution)/shard_map/reshape | solution.py:349
  1.8 2.1 %fusion.2 = (f32[480,128]{1,0:T(8,128)}, f32[480,128]{1,0:T(8,128)S(1)}, f32[480,128]{1,0:T(8,128)S(1)}, f32[480,128]{1,0:T(8,128)S(1)}) fusion(f32[60,32,128]{2,1,0:T(8,128)} %bitcast.28, f32[60,32,128]{2,1,0:T(8,128)} %bitcast.76, f32[8,128]{1,0:T(8,128)S(1)} %get-tuple-element.25, f32[8,128]{1,0:T(8,128)S(1)} %get-tuple-element.24), kind=kLoop, calls=%fused_computation.3 | loop fusion | flops 245760 | bytes 1974272 | tf_op jit(solution)/shard_map/reshape | solution.py:363
  3.9 2.6 %collective-permute-start.3 = (f32[480,128]{1,0:T(8,128)S(1)}, f32[480,128]{1,0:T(8,128)S(1)}, u32[]{:S(2)}, u32[]{:S(2)}) collective-permute-start(f32[480,128]{1,0:T(8,128)S(1)} %get-tuple-element.22.prev.cur.refs_6_.nxt), channel_id=1, source_target_pairs={{0,30},{2,4},{4,2},{6,8},{8,6},{10,12},{12,10},{14,16},{16,14},{18... | collective-permute-start | bytes 737288 | tf_op jit(solution)/shard_map/ppermute | solution.py:326
  6.5 1.7 %collective-permute-start.5 = (f32[480,128]{1,0:T(8,128)S(1)}, f32[480,128]{1,0:T(8,128)S(1)}, u32[]{:S(2)}, u32[]{:S(2)}) collective-permute-start(f32[480,128]{1,0:T(8,128)S(1)} %get-tuple-element.21.nxt.cur.refs_6_.prev), channel_id=1, source_target_pairs={{0,30},{2,4},{4,2},{6,8},{8,6},{10,12},{12,10},{14,16},{16,14},{18... | collective-permute-start | bytes 737288 | tf_op jit(solution)/shard_map/ppermute | solution.py:326
  8.3 11.9 %collective-permute-done.3.far = f32[480,128]{1,0:T(8,128)S(1)} collective-permute-done((f32[480,128]{1,0:T(8,128)S(1)}, f32[480,128]{1,0:T(8,128)S(1)}, u32[]{:S(2)}, u32[]{:S(2)}) %collective-permute-start.3) | collective-permute-done | bytes 245792 | tf_op jit(solution)/shard_map/ppermute | solution.py:326
  20.4 1.3 %collective-permute-start.4 = (f32[480,128]{1,0:T(8,128)S(1)}, f32[480,128]{1,0:T(8,128)}, u32[]{:S(2)}, u32[]{:S(2)}) collective-permute-start(f32[480,128]{1,0:T(8,128)S(1)} %lap.10.refs_7_), channel_id=1, source_target_pairs={{0,1},{1,0},{2,3},{3,2},{4,5},{5,4},{6,7},{7,6},{8,9},{9,8},{10,11... | collective-permute-start | bytes 737288 | tf_op jit(solution)/shard_map/ppermute | solution.py:334
  21.6 2.2 %collective-permute-done.11.far = f32[480,128]{1,0:T(8,128)S(1)} collective-permute-done((f32[480,128]{1,0:T(8,128)S(1)}, f32[480,128]{1,0:T(8,128)S(1)}, u32[]{:S(2)}, u32[]{:S(2)}) %collective-permute-start.11) | collective-permute-done | bytes 245792 | tf_op jit(solution)/shard_map/ppermute | solution.py:326
  24.0 1.9 %collective-permute-start.12 = (f32[480,128]{1,0:T(8,128)S(1)}, f32[480,128]{1,0:T(8,128)S(1)}, u32[]{:S(2)}, u32[]{:S(2)}) collective-permute-start(f32[480,128]{1,0:T(8,128)S(1)} %lap.13.refs_7_), channel_id=1, source_target_pairs={{0,1},{1,0},{2,3},{3,2},{4,5},{5,4},{6,7},{7,6},{8,9},{9,8},{10,11... | collective-permute-start | bytes 737288 | tf_op jit(solution)/shard_map/ppermute | solution.py:334
  26.7 1.9 %collective-permute-start.6 = (f32[480,128]{1,0:T(8,128)S(1)}, f32[480,128]{1,0:T(8,128)S(1)}, u32[]{:S(2)}, u32[]{:S(2)}) collective-permute-start(f32[480,128]{1,0:T(8,128)S(1)} %lap.11.refs_7_), channel_id=1, source_target_pairs={{0,1},{1,0},{2,3},{3,2},{4,5},{5,4},{6,7},{7,6},{8,9},{9,8},{10,11... | collective-permute-start | bytes 737288 | tf_op jit(solution)/shard_map/ppermute | solution.py:334
  29.1 1.2 %lap.9.refs_7_ = f32[480,128]{1,0:T(8,128)S(1)} custom-call(f32[480,128]{1,0:T(8,128)S(1)} %get-tuple-element.22.prev.cur.refs_6_.nxt, f32[480,128]{1,0:T(8,128)S(1)} %get-tuple-element.23.cur.refs_6_.nxt.prev, f32[480,128]{1,0:T(8,128)S(1)} %get-tuple-element.21.nxt.cur.refs_6_.prev, f32[60,32,128]{2,1,0:T(8,128)S(1)} %collective-permute-done.near, ...), custom_call_target="tpu_custom_call" | custom-call | flops 737280 | bytes 1474560 | tf_op jit(solution)/shard_map/lap/pallas_call | solution.py:232
  30.3 1.8 %collective-permute-start.2 = (f32[480,128]{1,0:T(8,128)S(1)}, f32[480,128]{1,0:T(8,128)S(1)}, u32[]{:S(2)}, u32[]{:S(2)}) collective-permute-start(f32[480,128]{1,0:T(8,128)S(1)} %lap.9.refs_7_), channel_id=1, source_target_pairs={{0,1},{1,0},{2,3},{3,2},{4,5},{5,4},{6,7},{7,6},{8,9},{9,8},{10,11... | collective-permute-start | bytes 737288 | tf_op jit(solution)/shard_map/ppermute | solution.py:334
  32.6 1.5 %final.8.prev.cur.nxt.refs_6_ = f32[480,128]{1,0:T(8,128)S(1)} custom-call(f32[7,32,128]{2,1,0:T(8,128)S(1)} %bitcast.37, f32[32,128]{1,0:T(8,128)S(1)} %bitcast.50, f32[32,128]{1,0:T(8,128)S(1)} %bitcast.57, s32[32,128]{1,0:T(8,128)S(1)} %bitcast.64, bf16[2,896,192]{2,1,0:T(8,128)(2,1)S(1)} %coupling.1.matrices.refs_4_, f32[60,32,128]{2,1,0:T(8,128)S(1)} %bitcast.29, ...), custom_call_target="tpu_custom_call" | custom-call | flops 154828800 | bytes 1474560 | tf_op jit(solution)/shard_map/final/pallas_call | solution.py:284
  34.7 1.3 %collective-permute-start.16 = (f32[480,128]{1,0:T(8,128)S(1)}, f32[480,128]{1,0:T(8,128)S(1)}, u32[]{:S(2)}, u32[]{:S(2)}) collective-permute-start(f32[480,128]{1,0:T(8,128)S(1)} %final.8.prev.cur.nxt.refs_6_), channel_id=1, source_target_pairs={{0,30},{2,4},{4,2},{6,8},{8,6},{10,12},{12,10},{14,16},{16,14},{18... | collective-permute-start | bytes 737288 | tf_op jit(solution)/shard_map/ppermute | solution.py:326
  36.7 2.3 %collective-permute-done.7.refs_10_ = f32[480,128]{1,0:T(8,128)S(1)} collective-permute-done((f32[480,128]{1,0:T(8,128)}, f32[480,128]{1,0:T(8,128)S(1)}, u32[]{:S(2)}, u32[]{:S(2)}) %collective-permute-start.7) | collective-permute-done | bytes 245792 | tf_op jit(solution)/shard_map/ppermute | solution.py:334
  38.9 1.3 %collective-permute-start.18 = (f32[480,128]{1,0:T(8,128)S(1)}, f32[480,128]{1,0:T(8,128)S(1)}, u32[]{:S(2)}, u32[]{:S(2)}) collective-permute-start(f32[480,128]{1,0:T(8,128)S(1)} %final.10.nxt.prev.cur.refs_6_), channel_id=1, source_target_pairs={{0,2},{2,0},{4,6},{6,4},{8,10},{10,8},{12,14},{14,12},{16,18},{18,... | collective-permute-start | bytes 737288 | tf_op jit(solution)/shard_map/ppermute | solution.py:320
  40.3 2.6 %collective-permute-done.6.refs_9_ = f32[480,128]{1,0:T(8,128)S(1)} collective-permute-done((f32[480,128]{1,0:T(8,128)S(1)}, f32[480,128]{1,0:T(8,128)S(1)}, u32[]{:S(2)}, u32[]{:S(2)}) %collective-permute-start.6) | collective-permute-done | bytes 245792 | tf_op jit(solution)/shard_map/ppermute | solution.py:334
  43.7 0.9 %final.9.nxt.cur.prev.refs_10_ = f32[960,128]{1,0:T(8,128)S(1)} custom-call(f32[7,32,128]{2,1,0:T(8,128)S(1)} %bitcast.41, f32[32,128]{1,0:T(8,128)S(1)} %bitcast.52, f32[32,128]{1,0:T(8,128)S(1)} %bitcast.59, s32[32,128]{1,0:T(8,128)S(1)} %bitcast.66, bf16[2,896,192]{2,1,0:T(8,128)(2,1)S(1)} %coupling.1.matrices.refs_4_, f32[60,32,128]{2,1,0:T(8,128)S(1)} %bitcast.31, ...), custom_call_target="tpu_custom_call" | custom-call | flops 309657600 | bytes 1474560 | tf_op jit(solution)/shard_map/final/pallas_call | solution.py:284
  45.2 1.3 %collective-permute-start.14 = (f32[960,128]{1,0:T(8,128)S(1)}, f32[960,128]{1,0:T(8,128)S(1)}, u32[]{:S(2)}, u32[]{:S(2)}) collective-permute-start(f32[960,128]{1,0:T(8,128)S(1)} %final.9.nxt.cur.prev.refs_10_), channel_id=1, source_target_pairs={{0,30},{2,4},{4,2},{6,8},{8,6},{10,12},{12,10},{14,16},{16,14},{18... | collective-permute-start | bytes 1474568 | tf_op jit(solution)/shard_map/ppermute | solution.py:326
  47.6 2.1 %collective-permute-start.8 = (f32[480,128]{1,0:T(8,128)S(1)}, f32[480,128]{1,0:T(8,128)S(1)}, u32[]{:S(2)}, u32[]{:S(2)}) collective-permute-start(f32[480,128]{1,0:T(8,128)S(1)} %final.7.cur.prev.nxt.refs_6_), channel_id=1, source_target_pairs={{0,2},{2,0},{4,6},{6,4},{8,10},{10,8},{12,14},{14,12},{16,18},{18,... | collective-permute-start | bytes 737288 | tf_op jit(solution)/shard_map/ppermute | solution.py:320
  51.5 0.9 %collective-permute-start.20 = (f32[480,128]{1,0:T(8,128)S(1)}, f32[480,128]{1,0:T(8,128)S(1)}, u32[]{:S(2)}, u32[]{:S(2)}) collective-permute-start(f32[480,128]{1,0:T(8,128)S(1)} %lap.17.refs_7_), channel_id=1, source_target_pairs={{0,1},{1,0},{2,3},{3,2},{4,5},{5,4},{6,7},{7,6},{8,9},{9,8},{10,11... | collective-permute-start | bytes 737288 | tf_op jit(solution)/shard_map/ppermute | solution.py:334
  52.4 14.3 %collective-permute-done.9.far = f32[480,128]{1,0:T(8,128)S(1)} collective-permute-done((f32[480,128]{1,0:T(8,128)S(1)}, f32[480,128]{1,0:T(8,128)S(1)}, u32[]{:S(2)}, u32[]{:S(2)}) %collective-permute-start.9) | collective-permute-done | bytes 245792 | tf_op jit(solution)/shard_map/ppermute | solution.py:326
  69.2 1.4 %final.11 = (f32[60,32,128]{2,1,0:T(8,128)}, f32[60,32,128]{2,1,0:T(8,128)}) custom-call(f32[7,32,128]{2,1,0:T(8,128)S(1)} %bitcast.47, f32[32,128]{1,0:T(8,128)S(1)} %bitcast.54, f32[32,128]{1,0:T(8,128)S(1)} %bitcast.61, s32[32,128]{1,0:T(8,128)S(1)} %bitcast.68, bf16[2,896,192]{2,1,0:T(8,128)(2,1)S(1)} %coupling.1.matrices.refs_4_, ...), custom_call_target="tpu_custom_call" | custom-call | flops 154828800 | bytes 1474560 | tf_op jit(solution)/shard_map/final/pallas_call | solution.py:284
  70.6 1.4 %final.12 = (f32[60,32,128]{2,1,0:T(8,128)}, f32[60,32,128]{2,1,0:T(8,128)}) custom-call(f32[7,32,128]{2,1,0:T(8,128)S(1)} %bitcast.48, f32[32,128]{1,0:T(8,128)S(1)} %bitcast.55, f32[32,128]{1,0:T(8,128)S(1)} %bitcast.62, s32[32,128]{1,0:T(8,128)S(1)} %bitcast.69, ...), custom_call_target="tpu_custom_call", output_to_operand_aliasing={{0}: (10, {}), {1}: (11, {})} | custom-call | flops 154828800 | bytes 1474560 | tf_op jit(solution)/shard_map/final/pallas_call | solution.py:284
  72.0 2.3 %final.13 = (f32[60,32,128]{2,1,0:T(8,128)}, f32[60,32,128]{2,1,0:T(8,128)}) custom-call(f32[7,32,128]{2,1,0:T(8,128)S(1)} %bitcast.49, f32[32,128]{1,0:T(8,128)S(1)} %bitcast.56, f32[32,128]{1,0:T(8,128)S(1)} %bitcast.63, s32[32,128]{1,0:T(8,128)S(1)} %bitcast.70, ...), custom_call_target="tpu_custom_call", output_to_operand_aliasing={{0}: (13, {}), {1}: (14, {})} | custom-call | flops 309657600 | bytes 2949120 | tf_op jit(solution)/shard_map/final/pallas_call | solution.py:284
  (59 shorter events, 10.2 us)
Async XLA Ops:
  1.6 18.5 %collective-permute-start = (f32[60,32,128]{2,1,0:T(8,128)}, f32[60,32,128]{2,1,0:T(8,128)S(1)}, u32[]{:S(2)}, u32[]{:S(2)}) collective-permute-start(f32[60,32,128]{2,1,0:T(8,128)} %bitcast.75), channel_id=1, source_target_pairs={{0,2},{2,0},{4,6},{6,4},{8,10},{10,8},{12,14},{14,12},{16,18},{18,... | collective-permute-start | bytes 2949128 | tf_op jit(solution)/shard_map/ppermute | solution.py:320
  3.9 16.3 %collective-permute-start.3 = (f32[480,128]{1,0:T(8,128)S(1)}, f32[480,128]{1,0:T(8,128)S(1)}, u32[]{:S(2)}, u32[]{:S(2)}) collective-permute-start(f32[480,128]{1,0:T(8,128)S(1)} %get-tuple-element.22.prev.cur.refs_6_.nxt), channel_id=1, source_target_pairs={{0,30},{2,4},{4,2},{6,8},{8,6},{10,12},{12,10},{14,16},{16,14},{18... | collective-permute-start | bytes 737288 | tf_op jit(solution)/shard_map/ppermute | solution.py:326
  6.5 17.3 %collective-permute-start.11 = (f32[480,128]{1,0:T(8,128)S(1)}, f32[480,128]{1,0:T(8,128)S(1)}, u32[]{:S(2)}, u32[]{:S(2)}) collective-permute-start(f32[480,128]{1,0:T(8,128)S(1)} %slice_bitcast_fusion.prev.nxt.cur.refs_6_), channel_id=1, source_target_pairs={{0,30},{2,4},{4,2},{6,8},{8,6},{10,12},{12,10},{14,16},{16,14},{18... | collective-permute-start | bytes 737288 | tf_op jit(solution)/shard_map/ppermute | solution.py:326
  6.5 20.0 %collective-permute-start.5 = (f32[480,128]{1,0:T(8,128)S(1)}, f32[480,128]{1,0:T(8,128)S(1)}, u32[]{:S(2)}, u32[]{:S(2)}) collective-permute-start(f32[480,128]{1,0:T(8,128)S(1)} %get-tuple-element.21.nxt.cur.refs_6_.prev), channel_id=1, source_target_pairs={{0,30},{2,4},{4,2},{6,8},{8,6},{10,12},{12,10},{14,16},{16,14},{18... | collective-permute-start | bytes 737288 | tf_op jit(solution)/shard_map/ppermute | solution.py:326
  8.2 20.9 %collective-permute-start.1 = (f32[480,128]{1,0:T(8,128)S(1)}, f32[480,128]{1,0:T(8,128)}, u32[]{:S(2)}, u32[]{:S(2)}) collective-permute-start(f32[480,128]{1,0:T(8,128)S(1)} %get-tuple-element.23.cur.refs_6_.nxt.prev), channel_id=1, source_target_pairs={{0,30},{2,4},{4,2},{6,8},{8,6},{10,12},{12,10},{14,16},{16,14},{18... | collective-permute-start | bytes 737288 | tf_op jit(solution)/shard_map/ppermute | solution.py:326
  20.4 12.2 %collective-permute-start.4 = (f32[480,128]{1,0:T(8,128)S(1)}, f32[480,128]{1,0:T(8,128)}, u32[]{:S(2)}, u32[]{:S(2)}) collective-permute-start(f32[480,128]{1,0:T(8,128)S(1)} %lap.10.refs_7_), channel_id=1, source_target_pairs={{0,1},{1,0},{2,3},{3,2},{4,5},{5,4},{6,7},{7,6},{8,9},{9,8},{10,11... | collective-permute-start | bytes 737288 | tf_op jit(solution)/shard_map/ppermute | solution.py:334
  24.0 10.7 %collective-permute-start.12 = (f32[480,128]{1,0:T(8,128)S(1)}, f32[480,128]{1,0:T(8,128)S(1)}, u32[]{:S(2)}, u32[]{:S(2)}) collective-permute-start(f32[480,128]{1,0:T(8,128)S(1)} %lap.13.refs_7_), channel_id=1, source_target_pairs={{0,1},{1,0},{2,3},{3,2},{4,5},{5,4},{6,7},{7,6},{8,9},{9,8},{10,11... | collective-permute-start | bytes 737288 | tf_op jit(solution)/shard_map/ppermute | solution.py:334
  25.9 13.1 %collective-permute-start.7 = (f32[480,128]{1,0:T(8,128)}, f32[480,128]{1,0:T(8,128)S(1)}, u32[]{:S(2)}, u32[]{:S(2)}) collective-permute-start(f32[480,128]{1,0:T(8,128)} %get-tuple-element.20), channel_id=1, source_target_pairs={{0,1},{1,0},{2,3},{3,2},{4,5},{5,4},{6,7},{7,6},{8,9},{9,8},{10,11... | collective-permute-start | bytes 737288 | tf_op jit(solution)/shard_map/ppermute | solution.py:334
  26.4 2.1 %copy-start.6 = (f32[7,72]{1,0:T(8,128)S(1)}, f32[7,72]{1,0:T(8,128)}, u32[]{:S(2)}) copy-start(f32[7,72]{1,0:T(8,128)} %entries.1) | copy-start | bytes 6052
  26.7 16.2 %collective-permute-start.6 = (f32[480,128]{1,0:T(8,128)S(1)}, f32[480,128]{1,0:T(8,128)S(1)}, u32[]{:S(2)}, u32[]{:S(2)}) collective-permute-start(f32[480,128]{1,0:T(8,128)S(1)} %lap.11.refs_7_), channel_id=1, source_target_pairs={{0,1},{1,0},{2,3},{3,2},{4,5},{5,4},{6,7},{7,6},{8,9},{9,8},{10,11... | collective-permute-start | bytes 737288 | tf_op jit(solution)/shard_map/ppermute | solution.py:334
  29.0 3.0 %copy-start.1 = (f32[7,1,32,128]{3,2,1,0:T(8,128)S(1)}, f32[7,1,32,128]{3,2,1,0:T(8,128)}, u32[]{:S(2)}) copy-start(f32[7,1,32,128]{3,2,1,0:T(8,128)} %param.13) | copy-start | bytes 344068
  30.3 2.3 %copy-start = (f32[60,1,32,128]{3,2,1,0:T(8,128)S(1)}, f32[60,1,32,128]{3,2,1,0:T(8,128)}, u32[]{:S(2)}) copy-start(f32[60,1,32,128]{3,2,1,0:T(8,128)} %param.9) | copy-start | bytes 2949124
  30.3 15.0 %collective-permute-start.2 = (f32[480,128]{1,0:T(8,128)S(1)}, f32[480,128]{1,0:T(8,128)S(1)}, u32[]{:S(2)}, u32[]{:S(2)}) collective-permute-start(f32[480,128]{1,0:T(8,128)S(1)} %lap.9.refs_7_), channel_id=1, source_target_pairs={{0,1},{1,0},{2,3},{3,2},{4,5},{5,4},{6,7},{7,6},{8,9},{9,8},{10,11... | collective-permute-start | bytes 737288 | tf_op jit(solution)/shard_map/ppermute | solution.py:334
  34.2 11.1 %collective-permute-start.15 = (f32[480,128]{1,0:T(8,128)S(1)}, f32[480,128]{1,0:T(8,128)S(1)}, u32[]{:S(2)}, u32[]{:S(2)}) collective-permute-start(f32[480,128]{1,0:T(8,128)S(1)} %final.8.prev.cur.nxt.refs_6_), channel_id=1, source_target_pairs={{0,2},{2,0},{4,6},{6,4},{8,10},{10,8},{12,14},{14,12},{16,18},{18,... | collective-permute-start | bytes 737288 | tf_op jit(solution)/shard_map/ppermute | solution.py:320
  34.7 12.9 %collective-permute-start.16 = (f32[480,128]{1,0:T(8,128)S(1)}, f32[480,128]{1,0:T(8,128)S(1)}, u32[]{:S(2)}, u32[]{:S(2)}) collective-permute-start(f32[480,128]{1,0:T(8,128)S(1)} %final.8.prev.cur.nxt.refs_6_), channel_id=1, source_target_pairs={{0,30},{2,4},{4,2},{6,8},{8,6},{10,12},{12,10},{14,16},{16,14},{18... | collective-permute-start | bytes 737288 | tf_op jit(solution)/shard_map/ppermute | solution.py:326
  38.9 10.8 %collective-permute-start.18 = (f32[480,128]{1,0:T(8,128)S(1)}, f32[480,128]{1,0:T(8,128)S(1)}, u32[]{:S(2)}, u32[]{:S(2)}) collective-permute-start(f32[480,128]{1,0:T(8,128)S(1)} %final.10.nxt.prev.cur.refs_6_), channel_id=1, source_target_pairs={{0,2},{2,0},{4,6},{6,4},{8,10},{10,8},{12,14},{14,12},{16,18},{18,... | collective-permute-start | bytes 737288 | tf_op jit(solution)/shard_map/ppermute | solution.py:320
  42.9 7.7 %collective-permute-start.19 = (f32[480,128]{1,0:T(8,128)S(1)}, f32[480,128]{1,0:T(8,128)S(1)}, u32[]{:S(2)}, u32[]{:S(2)}) collective-permute-start(f32[480,128]{1,0:T(8,128)S(1)} %final.10.nxt.prev.cur.refs_6_), channel_id=1, source_target_pairs={{0,30},{2,4},{4,2},{6,8},{8,6},{10,12},{12,10},{14,16},{16,14},{18... | collective-permute-start | bytes 737288 | tf_op jit(solution)/shard_map/ppermute | solution.py:326
  45.2 23.6 %collective-permute-start.13 = (f32[960,128]{1,0:T(8,128)S(1)}, f32[960,128]{1,0:T(8,128)S(1)}, u32[]{:S(2)}, u32[]{:S(2)}) collective-permute-start(f32[960,128]{1,0:T(8,128)S(1)} %final.9.nxt.cur.prev.refs_10_), channel_id=1, source_target_pairs={{0,2},{2,0},{4,6},{6,4},{8,10},{10,8},{12,14},{14,12},{16,18},{18,... | collective-permute-start | bytes 1474568 | tf_op jit(solution)/shard_map/ppermute | solution.py:320
  45.2 23.6 %collective-permute-start.14 = (f32[960,128]{1,0:T(8,128)S(1)}, f32[960,128]{1,0:T(8,128)S(1)}, u32[]{:S(2)}, u32[]{:S(2)}) collective-permute-start(f32[960,128]{1,0:T(8,128)S(1)} %final.9.nxt.cur.prev.refs_10_), channel_id=1, source_target_pairs={{0,30},{2,4},{4,2},{6,8},{8,6},{10,12},{12,10},{14,16},{16,14},{18... | collective-permute-start | bytes 1474568 | tf_op jit(solution)/shard_map/ppermute | solution.py:326
  47.6 3.8 %collective-permute-start.8 = (f32[480,128]{1,0:T(8,128)S(1)}, f32[480,128]{1,0:T(8,128)S(1)}, u32[]{:S(2)}, u32[]{:S(2)}) collective-permute-start(f32[480,128]{1,0:T(8,128)S(1)} %final.7.cur.prev.nxt.refs_6_), channel_id=1, source_target_pairs={{0,2},{2,0},{4,6},{6,4},{8,10},{10,8},{12,14},{14,12},{16,18},{18,... | collective-permute-start | bytes 737288 | tf_op jit(solution)/shard_map/ppermute | solution.py:320
  49.7 17.0 %collective-permute-start.9 = (f32[480,128]{1,0:T(8,128)S(1)}, f32[480,128]{1,0:T(8,128)S(1)}, u32[]{:S(2)}, u32[]{:S(2)}) collective-permute-start(f32[480,128]{1,0:T(8,128)S(1)} %final.7.cur.prev.nxt.refs_6_), channel_id=1, source_target_pairs={{0,30},{2,4},{4,2},{6,8},{8,6},{10,12},{12,10},{14,16},{16,14},{18... | collective-permute-start | bytes 737288 | tf_op jit(solution)/shard_map/ppermute | solution.py:326
  50.6 18.4 %collective-permute-start.17 = (f32[608,128]{1,0:T(8,128)S(1)}, f32[608,128]{1,0:T(8,128)S(1)}, u32[]{:S(2)}, u32[]{:S(2)}) collective-permute-start(f32[608,128]{1,0:T(8,128)S(1)} %lap.15.refs_7_), channel_id=1, source_target_pairs={{0,1},{1,0},{2,3},{3,2},{4,5},{5,4},{6,7},{7,6},{8,9},{9,8},{10,11... | collective-permute-start | bytes 933896 | tf_op jit(solution)/shard_map/ppermute | solution.py:334
  51.5 19.1 %collective-permute-start.20 = (f32[480,128]{1,0:T(8,128)S(1)}, f32[480,128]{1,0:T(8,128)S(1)}, u32[]{:S(2)}, u32[]{:S(2)}) collective-permute-start(f32[480,128]{1,0:T(8,128)S(1)} %lap.17.refs_7_), channel_id=1, source_target_pairs={{0,1},{1,0},{2,3},{3,2},{4,5},{5,4},{6,7},{7,6},{8,9},{9,8},{10,11... | collective-permute-start | bytes 737288 | tf_op jit(solution)/shard_map/ppermute | solution.py:334
  66.9 5.1 %collective-permute-start.10 = (f32[480,128]{1,0:T(8,128)S(1)}, f32[480,128]{1,0:T(8,128)S(1)}, u32[]{:S(2)}, u32[]{:S(2)}) collective-permute-start(f32[480,128]{1,0:T(8,128)S(1)} %lap.12.refs_7_), channel_id=1, source_target_pairs={{0,1},{1,0},{2,3},{3,2},{4,5},{5,4},{6,7},{7,6},{8,9},{9,8},{10,11... | collective-permute-start | bytes 737288 | tf_op jit(solution)/shard_map/ppermute | solution.py:334
  (4 other events, 5.2 us)
